TPU v7x, 32 devices: a whole 2x2x4 slice. The times are simulated.
32 devices in a mesh: groups: 2 (over y), seq: 4 (over z), heads: 2 (over x), cfg: 2 (over core).
Axes of the slice: x: 2, y: 2, z: 4, core: 2. Of those that a mesh axis runs over, the one named last changes fastest.
Arguments:
- video_tokens: bfloat16 [2, 8, 1152, 1024], P('cfg', ('groups', 'seq'), 'heads'), parts along dimension 1, may hold values from -6 to 6
- text_tokens: bfloat16 [2, 8, 1152, 128], P('cfg', ('groups', 'seq'), 'heads'), parts along dimension 1, may hold values from -6 to 6
- text_length: int32 [2, 8], P('cfg', ('groups', 'seq')), parts along dimension 1, may hold values from 1 to 128
- guide_numer: int32 [8], P(('groups', 'seq')), parts along dimension 0, may hold values from 2 to 8
- guide_denom: int32 [8], P(('groups', 'seq')), parts along dimension 0, may hold values from 4 to 8
- spatial_gain: bfloat16 [1152], replicated, may hold values from 0.25 to 1.75
- spatial_qkv: bfloat16 [3, 1152, 1152], P(None, 'heads'), may hold values from -0.11785113 to 0.11785113
- spatial_out: bfloat16 [1152, 1152], P('heads'), may hold values from -0.1875 to 0.1875
- temporal_gain: bfloat16 [1152], replicated, may hold values from 0.25 to 1.75
- temporal_qkv: bfloat16 [3, 1152, 1152], P(None, 'heads'), may hold values from -0.11785113 to 0.11785113
- temporal_out: bfloat16 [1152, 1152], P('heads'), may hold values from -0.1875 to 0.1875
Outputs:
- guided: bfloat16 [8, 1152, 1024], P(('groups', 'seq'), ('heads', 'cfg')), parts along dimension 0
There are 2 independent parts, one for each index of `groups`. A program takes and returns all parts, laid end to end along the dimension named above; an argument that names none is the same for every part. Nothing has to cross between parts.
Inputs may be any that keep to these rules, and one draw needn't show every extreme that they name: `text_length`: text tokens at or beyond a frame's length are padding.
All inputs are finite; a program needn't handle non-finite values.
Results may differ from a plain program's by a relative error of at most 0.009.
Values may be sent and summed in bfloat16 or wider, within the bound.
No kernel may reach another device: no remote copies, remote signals or barrier semaphores. Data moves between devices by JAX's collectives and lax.ppermute only.
A program may use at most 64 MiB of HBM per device.

v0:
```python
import functools

import jax
import jax.numpy as jnp
from jax import lax
from jax.experimental import pallas as pl
from jax.experimental.pallas import tpu as pltpu
from jax.sharding import PartitionSpec as P

D = 1152
HEAD_DIM = 72
HEAD_ROWS = 80
LANES = 128
HEADS, SEQ, GROUPS, CFG = "heads", "seq", "groups", "cfg"


epsilon = 1e-06


def from_partner(shard, axis, stride):
    return lax.ppermute(shard, axis, [(i, i ^ 1 << stride) for i in range(lax.axis_size(axis))])


def softmax_along(scores, axis):
    top_score = jnp.max(scores, axis=axis, keepdims=True)
    expons = jnp.exp(scores - top_score)
    return (expons / jnp.sum(expons, axis=axis, keepdims=True)).astype(jnp.bfloat16)


def project_piece(piece, gain_vector, weights, parts):
    gain_piece = gain_vector.astype(jnp.float32)
    weight_piece = weights[parts]
    piece_wide = piece.astype(jnp.float32)
    scaled = (piece_wide * gain_piece[None, :, None]).astype(jnp.bfloat16)
    product = jnp.einsum("kod,fdp->fkop", weight_piece, scaled, preferred_element_type=jnp.float32)
    return (product, jnp.sum(piece_wide * piece_wide, axis=1))


def add_mixed(piece, matrix):
    return jnp.einsum("oc,fcp->fop", matrix, piece, preferred_element_type=jnp.float32)


def shards_plain(
    video_tokens,
    text_tokens,
    text_length,
    guide_numer,
    guide_denom,
    spatial_gain,
    spatial_qkv,
    spatial_out,
    temporal_gain,
    temporal_qkv,
    temporal_out,
):
    frame_count = video_tokens.shape[1]
    width = video_tokens.shape[2]
    positions = video_tokens.shape[3]
    text_count = text_tokens.shape[3]
    local_heads = width // HEAD_DIM
    frame_tokens = video_tokens[0]
    frame_text = text_tokens[0]
    video_piece = lax.all_gather(frame_tokens, HEADS, axis=1, tiled=True)
    text_piece = lax.all_gather(frame_text, HEADS, axis=1, tiled=True)
    video_add, video_sq = project_piece(video_piece, spatial_gain, spatial_qkv, slice(0, 3))
    text_add, text_sq = project_piece(text_piece, spatial_gain, spatial_qkv, slice(1, 3))
    mixed = (video_add * lax.rsqrt(video_sq / D + epsilon)[:, None, None, :]).astype(jnp.bfloat16)
    mixed = mixed.reshape(frame_count, 3, local_heads, HEAD_DIM, positions)
    context = (text_add * lax.rsqrt(text_sq / D + epsilon)[:, None, None, :]).astype(jnp.bfloat16)
    context = context.reshape(frame_count, 2, local_heads, HEAD_DIM, text_count)
    key_rows = jnp.concatenate([mixed[:, 1], context[:, 0]], axis=3)
    value_rows = jnp.concatenate([mixed[:, 2], context[:, 1]], axis=3)
    query_all = mixed[:, 0]
    text_valid = jnp.arange(text_count, dtype=jnp.int32)[None, :] < text_length[0][:, None]
    valid_keys = jnp.concatenate(
        [jnp.ones((frame_count, positions), dtype=bool), text_valid], axis=1
    )
    block_rows = min(512, positions)
    block_count = positions // block_rows
    frame_ids = jnp.repeat(jnp.arange(frame_count, dtype=jnp.int32), block_count)
    block_ids = jnp.tile(jnp.arange(block_count, dtype=jnp.int32), frame_count)

    def block_step(inputs):
        frame_id, block_id = inputs
        query_rows = lax.dynamic_slice_in_dim(
            query_all[frame_id], block_id * block_rows, block_rows, 2
        )
        scores = jnp.einsum(
            "hep,hek->hpk", query_rows, key_rows[frame_id], preferred_element_type=jnp.float32
        )
        scores = scores * HEAD_DIM ** (-0.5)
        scores = jnp.where(valid_keys[frame_id][None, None, :], scores, -jnp.inf)
        weights = softmax_along(scores, 2)
        result = jnp.einsum(
            "hpk,hek->hep", weights, value_rows[frame_id], preferred_element_type=jnp.float32
        )
        return result.astype(jnp.bfloat16)

    attended = lax.map(block_step, (frame_ids, block_ids))
    attended = attended.reshape(frame_count, block_count, local_heads, HEAD_DIM, block_rows)
    attended = jnp.transpose(attended, (0, 2, 3, 1, 4)).reshape(frame_count, width, positions)
    update = add_mixed(lax.all_gather(attended, HEADS, axis=1, tiled=True), spatial_out)
    after_spatial = (frame_tokens.astype(jnp.float32) + update).astype(jnp.bfloat16)
    own_rows = lax.all_to_all(after_spatial, SEQ, split_axis=2, concat_axis=0, tiled=True)
    frames_all = own_rows.shape[0]
    columns = own_rows.shape[2]
    piece_add, piece_sq = project_piece(
        lax.all_gather(own_rows, HEADS, axis=1, tiled=True),
        temporal_gain,
        temporal_qkv,
        slice(0, 3),
    )
    mixed_time = (piece_add * lax.rsqrt(piece_sq / D + epsilon)[:, None, None, :]).astype(
        jnp.bfloat16
    )
    mixed_time = mixed_time.reshape(frames_all, 3, local_heads, HEAD_DIM, columns)
    time_scores = jnp.einsum(
        "fhep,ghep->hfgp", mixed_time[:, 0], mixed_time[:, 1], preferred_element_type=jnp.float32
    )
    time_weights = softmax_along(time_scores * HEAD_DIM ** (-0.5), 2)
    attended_time = jnp.einsum(
        "hfgp,ghep->fhep", time_weights, mixed_time[:, 2], preferred_element_type=jnp.float32
    )
    attended_time = attended_time.astype(jnp.bfloat16).reshape(frames_all, width, columns)
    update_time = add_mixed(
        lax.all_gather(attended_time, HEADS, axis=1, tiled=True), temporal_out
    )
    block_out = (own_rows.astype(jnp.float32) + update_time).astype(jnp.bfloat16)
    returned = lax.all_to_all(block_out, SEQ, split_axis=0, concat_axis=2, tiled=True)
    half_width = width // 2
    partner = from_partner(returned, CFG, 0)
    branch_index = lax.axis_index(CFG)
    cond_full = jnp.where(branch_index == 0, returned, partner)
    uncond_full = jnp.where(branch_index == 0, partner, returned)
    cond_part = lax.dynamic_slice_in_dim(cond_full, branch_index * half_width, half_width, 1)
    uncond_part = lax.dynamic_slice_in_dim(uncond_full, branch_index * half_width, half_width, 1)
    ratio = guide_numer.astype(jnp.float32) / guide_denom.astype(jnp.float32)
    cond_wide = cond_part.astype(jnp.float32)
    uncond_wide = uncond_part.astype(jnp.float32)
    return (uncond_wide + ratio[:, None, None] * (cond_wide - uncond_wide)).astype(jnp.bfloat16)


def fits(mesh):
    heads = mesh.shape[HEADS]
    share = mesh.shape[GROUPS] * mesh.shape[CFG]
    return (D // (heads * share)) % (2 * HEAD_DIM) == 0


def aligned(offset, step=16):
    return pl.multiple_of(offset, step)


def local(x):
    return pltpu.with_memory_space_constraint(x, pltpu.VMEM)


def resident(kernel, shapes, info, operands, scratch, flops, grant, exps=0, out_local=True):
    place = pl.BlockSpec(memory_space=pltpu.VMEM)
    kind = pltpu.VMEM if out_local else jax.ShapeDtypeStruct
    moved = sum(x.size * x.dtype.itemsize for x in operands)
    return pl.pallas_call(
        kernel,
        out_shape=tuple(kind(shape, dtype) for shape, dtype in shapes),
        in_specs=[pl.BlockSpec(memory_space=pltpu.SMEM)] + [place] * len(operands),
        out_specs=(place,) * len(shapes),
        scratch_shapes=scratch,
        compiler_params=pltpu.CompilerParams(vmem_limit_bytes=grant << 20),
        cost_estimate=pl.CostEstimate(flops=flops, bytes_accessed=moved, transcendentals=exps),
    )(info, *[local(x) for x in operands])


def place_of(axis):
    return lax.axis_index(axis)


def base_of(heads, r, width):
    return lax.rem(place_of(HEADS) - r + heads, heads) * width


def quarter_of(block, rows, groups, cfg):
    _, dg, dc = block
    g = lax.rem(place_of(GROUPS) - dg + groups, groups)
    return (g * cfg + lax.rem(place_of(CFG) - dc + cfg, cfg)) * rows


def weave(y, inverse, tail):
    heads = y.shape[0] // HEAD_DIM
    y = (y * inverse).reshape(heads, HEAD_DIM, y.shape[1])
    return jnp.concatenate([y, jnp.broadcast_to(tail, (heads,) + tail.shape)], axis=1)


def project_kernel(parts, jobs, info, *refs):
    inputs, refs = refs[: parts * len(jobs)], refs[parts * len(jobs) :]
    gain, w, refs = refs[0], refs[1], refs[2:]
    outs, scaled_refs = refs[: len(jobs)], refs[len(jobs) :]
    width = w.shape[1]
    for i, kinds in enumerate(jobs):
        scaled, total = scaled_refs[i], None
        for r in range(parts):
            rows = pl.ds(aligned(base_of(parts, r, width)), width)
            wide = inputs[i * parts + r][...].astype(jnp.float32)
            scaled[rows, :] = (wide * gain[rows, :]).astype(jnp.bfloat16)
            sq = jnp.sum(wide * wide, axis=0, keepdims=True)
            total = sq if total is None else total + sq
        inverse = lax.rsqrt(total / D + epsilon)
        row = lax.broadcasted_iota(
            jnp.int32, (HEAD_ROWS - HEAD_DIM, scaled.shape[1]), 0
        )
        for slot, kind in enumerate(kinds):
            y = jnp.dot(w[kind], scaled[...], preferred_element_type=jnp.float32)
            tail = jnp.where((row == 0) & (kind == 2), 1.0, 0.0)
            rate = HEAD_DIM ** (-0.5) * 1.4426950408889634 if kind == 0 else 1.0
            outs[i][slot] = weave(y, inverse * rate, tail).astype(jnp.bfloat16)


def project_call(info, sets, jobs, gain, w):
    width = w.shape[1]
    heads = width // HEAD_DIM
    parts = len(sets[0])
    counts = [x[0].shape[1] for x in sets]
    shapes = [
        ((len(kinds), heads, HEAD_ROWS, n), jnp.bfloat16) for kinds, n in zip(jobs, counts)
    ]
    return resident(
        functools.partial(project_kernel, parts, jobs),
        shapes,
        info,
        [x for group in sets for x in group] + [gain, w],
        [pltpu.VMEM((D, n), jnp.bfloat16) for n in counts],
        6 * width * D * sum(counts),
        12,
    )


def crossing(seq, cross):
    half = lax.div(place_of(SEQ), seq // 2)
    return 1 - half if cross else half


def pick_chunk(chunks, index, read):
    value = read(chunks[0])
    for i in range(1, len(chunks)):
        value = jnp.where(index == i, read(chunks[i]), value)
    return value


def attend_kernel(parts, aheads, count, with_text, resumed, final, info, *refs):
    queries, refs = refs[:parts], refs[parts:]
    keys, refs = list(refs[:count]), refs[count:]
    text = None
    if with_text:
        text, refs = refs[0], refs[1:]
    states, refs = refs[: 2 * len(aheads) * resumed], refs[2 * len(aheads) * resumed :]
    outs, (s_buf, m_buf, *o_buf) = refs[: len(aheads) * (2 - final)], refs[len(aheads) * (2 - final) :]
    heads, block = keys[0].shape[1], keys[0].shape[3]
    contract = (((0,), (0,)), ((), ()))

    def fold(s):
        return jnp.max(s.reshape(s.shape[0] // 8, 8, s.shape[1]), axis=0)

    group = s_buf.shape[1] // len(aheads)
    items = [(n, u) for n in range(len(aheads)) for u in range(group)]

    def score(stage, slot):
        for j, (n, u) in enumerate(items):
            head = stage * group + u
            index = lax.rem(place_of(HEADS) + aheads[n], parts)
            q = pick_chunk(queries, index, lambda chunk: chunk[0, head])
            top = None
            for i, chunk in enumerate(keys):
                s = lax.dot_general(
                    chunk[1, head], q, contract, preferred_element_type=jnp.float32
                )
                s_buf[slot, j, i * block : (i + 1) * block, :] = s
                top = fold(s) if top is None else jnp.maximum(top, fold(s))
            if with_text:
                t = lax.dot_general(
                    text[0, head], q, contract, preferred_element_type=jnp.float32
                )
                live = lax.broadcasted_iota(jnp.int32, t.shape, 0) < info[0]
                t = jnp.where(live, t, -jnp.inf)
                s_buf[slot, j, count * block :, :] = t
                top = jnp.maximum(top, fold(t))
            m_buf[slot, j] = top

    def mix(stage, slot):
        for j, (n, u) in enumerate(items):
            head = stage * group + u
            top = jnp.max(m_buf[slot, j], axis=0, keepdims=True)
            o = None
            if resumed:
                before = states[2 * n + 1][head, 0:1, :]
                top = jnp.maximum(top, before)
                o = states[2 * n][head] * jnp.exp2(before - top)
            for i in range(count + with_text):
                if i < count:
                    s, v = s_buf[slot, j, i * block : (i + 1) * block, :], keys[i][2, head]
                else:
                    s, v = s_buf[slot, j, count * block :, :], text[1, head]
                e = jnp.exp2(s - top).astype(jnp.bfloat16)
                term = jnp.dot(v, e, preferred_element_type=jnp.float32)
                o = term if o is None else o + term
            if final:
                rows = pl.ds(aligned(head * HEAD_DIM, 8), HEAD_DIM)
                o_buf[n][rows, :] = o[:HEAD_DIM] / o[HEAD_DIM : HEAD_DIM + 1]
            else:
                outs[2 * n][head] = o
                outs[2 * n + 1][head] = jnp.broadcast_to(top, (8, block))

    stages = heads // group
    score(0, 0)

    def step(i, carry):
        score(2 * i + 1, 1)
        mix(2 * i, 0)
        score(2 * i + 2, 0)
        mix(2 * i + 1, 1)
        return carry

    lax.fori_loop(0, stages // 2 - 1, step, 0)
    score(stages - 1, 1)
    mix(stages - 2, 0)
    mix(stages - 1, 1)
    if final:
        for n in range(len(aheads)):
            outs[n][...] = o_buf[n][...].astype(jnp.bfloat16)


def attend_call(info, queries, keys, text, states, aheads, final):
    parts, count = len(queries), len(keys)
    _, heads, _, block = keys[0].shape
    rows = block * count + (text.shape[3] if text is not None else 0)
    items = len(aheads) * (2 if count == 1 and heads % 4 == 0 else 1)
    if final:
        shapes = [((heads * HEAD_DIM, block), jnp.bfloat16)] * len(aheads)
        extra = [pltpu.VMEM((heads * HEAD_DIM, block), jnp.float32)] * len(aheads)
    else:
        shapes = [
            ((heads, HEAD_ROWS, block), jnp.float32),
            ((heads, 8, block), jnp.float32),
        ] * len(aheads)
        extra = []
    return resident(
        functools.partial(
            attend_kernel,
            parts,
            aheads,
            count,
            int(text is not None),
            int(bool(states)),
            int(final),
        ),
        shapes,
        info,
        list(queries) + list(keys) + ([text] if text is not None else []) + list(states),
        [
            pltpu.VMEM((2, items, rows, block), jnp.float32),
            pltpu.VMEM((2, items, 8, block), jnp.float32),
        ]
        + extra,
        4 * heads * 256 * block * rows * len(aheads),
        12,
        heads * block * rows * len(aheads),
    )


def out_kernel(n, extra, seq, blocks, share, info, *refs):
    att, refs = refs[:n], refs[n:]
    tokens, refs = refs[: n * len(blocks)], refs[n * len(blocks) :]
    w, refs = refs[: len(blocks)], refs[len(blocks) :]
    outs, (a, held) = refs[:-2], refs[-2:]
    width = att[0].shape[0]
    lanes = outs[0].shape[1]
    index = place_of(HEADS)
    skip = 0 if extra else width
    for r in range(n):
        a[pl.ds(aligned(base_of(n, r, width)), width), :] = att[r][...]
    far_w = [w[b][...] for b, key in enumerate(blocks) if key[0]]
    if far_w:
        far_y = jnp.dot(
            jnp.concatenate(far_w, axis=0), a[...], preferred_element_type=jnp.float32
        )
    done = 0
    for b, key in enumerate(blocks):
        count = w[b].shape[0]
        if key[0]:
            y = far_y[done : done + count]
            done += count
            offset = aligned(quarter_of(key, count, *share))
            inner, rows = pl.ds(offset, count), pl.ds(aligned(key[0] * width - skip + offset), count)
        else:
            y = jnp.dot(w[b][...], a[...], preferred_element_type=jnp.float32)
            inner, rows = slice(0, width), slice(0, width)
        x = pick_chunk(tokens[b * n : (b + 1) * n], index, lambda t: t[inner, :])
        held[rows, :] = (x.astype(jnp.float32) + y).astype(jnp.bfloat16)
    row = lax.broadcasted_iota(jnp.int32, (16, lanes), 0)
    numer, denom = info[1].astype(jnp.float32), info[2].astype(jnp.float32)
    tail = jnp.where(row == 0, numer, jnp.where(row == 1, denom, 0.0)).astype(jnp.bfloat16)
    outs = list(outs)
    for start, stop in [(0, width)] * bool(extra) + [(width, D)] * (held.shape[0] > width or not extra):
        for m in range(seq // 2):
            out = outs.pop(0)
            dest = lax.rem(lax.rem(place_of(SEQ), seq // 2) + m, seq // 2)
            span = pl.ds(aligned(dest * lanes, LANES), lanes)
            out[0 : stop - start, :] = held[start - skip : stop - skip, span]
            if start == 0:
                out[stop:, :] = tail


def out_call(info, att, tokens, w, extra, seq, blocks, share):
    n = len(att)
    width, count = att[0].shape
    total = sum(x.shape[0] for x in w)
    own = [((width + extra, 2 * count // seq), jnp.bfloat16)] * (seq // 2)
    other = [((D - width, 2 * count // seq), jnp.bfloat16)] * (seq // 2)
    return resident(
        functools.partial(out_kernel, n, extra, seq, blocks, share),
        own * bool(extra) + other * (total > width or not extra),
        info,
        list(att) + [x for group in tokens for x in group] + list(w),
        [pltpu.VMEM((D, count), jnp.bfloat16), pltpu.VMEM((total, count), jnp.bfloat16)],
        2 * D * total * count,
        12,
    )


def time_attend(read, att, rows, frames, heads):
    query, key, value = [
        [read(kind, f).reshape(heads, HEAD_DIM, read(kind, f).shape[1]) for f in range(frames)]
        for kind in range(3)
    ]
    lanes = query[0].shape[2]
    for f in range(frames):
        scores = [
            jnp.sum(query[f] * key[g], axis=1, keepdims=True) * HEAD_DIM ** (-0.5)
            for g in range(frames)
        ]
        top = functools.reduce(jnp.maximum, scores)
        expons = [jnp.exp(x - top) for x in scores]
        bottom = functools.reduce(jnp.add, expons)
        result = None
        for g in range(frames):
            weight = (expons[g] / bottom).astype(jnp.bfloat16).astype(jnp.float32)
            term = weight * value[g]
            result = term if result is None else result + term
        att[rows, f * lanes : (f + 1) * lanes] = result.reshape(
            heads * HEAD_DIM, lanes
        ).astype(jnp.bfloat16)


def time_project(near, far, gain, w, xs, inverse, out, parts, done=None):
    lanes = near[0].shape[1]
    width = w.shape[1]
    for f in range(len(near)):
        cols = slice(f * lanes, (f + 1) * lanes)
        total = None
        for r in range(parts):
            base = base_of(parts, r, width)
            if r == 0:
                x = near[f][0:width, :]
            else:
                x = far[f][(r - 1) * width : r * width, :]
            x = x.astype(jnp.float32)
            xs[pl.ds(aligned(base), width), cols] = (
                x * gain[pl.ds(aligned(D + base), width), :]
            ).astype(jnp.bfloat16)
            sq = jnp.sum(x * x, axis=0, keepdims=True)
            total = sq if total is None else total + sq
        inverse[:, cols] = jnp.broadcast_to(lax.rsqrt(total / D + epsilon), (8, lanes))
    for top in range(0, width, width // 2):
        span = slice(top, top + width // 2)
        for kind in range(3):
            y = jnp.dot(w[kind, span, :], xs[...], preferred_element_type=jnp.float32)
            out[kind, span, :] = (y * inverse[0:1, :]).astype(jnp.bfloat16)
        if done is not None:
            done(span)


def time_cross_kernel(frames, parts, info, *refs):
    near, far, refs = refs[:frames], refs[frames : 2 * frames], refs[2 * frames :]
    gain, w, xs, inverse, out = refs
    time_project(near, far, gain, w, xs, inverse, out, parts)


def time_near_kernel(frames, parts, share, info, *refs):
    near, far, refs = refs[:frames], refs[frames : 2 * frames], refs[2 * frames :]
    gain, w, crossed, xs, inverse, att, out = refs
    lanes = near[0].shape[1]
    rows = w.shape[1] // share

    def attend(part):
        for top in range(part.start, part.stop, rows):
            span = slice(top, top + rows)

            def read(kind, f):
                source = out if f < frames else crossed
                start = f % frames * lanes
                return source[kind, span, start : start + lanes].astype(jnp.float32)

            time_attend(read, att, span, 2 * frames, rows // HEAD_DIM)

    time_project(near, far, gain, w, xs, inverse, out, parts, attend)


def time_far_kernel(frames, share, keys, width, info, *refs):
    sides, refs = (refs[0:2], refs[2:4]), refs[4:]
    w, att = refs[:-1], refs[-1]
    rows = w[0].shape[0]
    half = frames // 2
    lanes = att.shape[1] // frames
    for b, key in enumerate(keys):
        span = pl.ds(aligned((key[0] - 1) * width + quarter_of(key, rows, *share)), rows)
        made = []
        for kind in range(3):
            part = w[2 * b][...] if kind == 0 else w[2 * b + 1][(kind - 1) * rows : kind * rows, :]
            for xs, inverse in sides:
                y = jnp.dot(part, xs[...], preferred_element_type=jnp.float32)
                made.append((y * inverse[0:1, :]).astype(jnp.bfloat16).astype(jnp.float32))

        def read(kind, f):
            start = f % half * lanes
            return made[2 * kind + f // half][:, start : start + lanes]

        time_attend(read, att, span, frames, rows // HEAD_DIM)


def time_cross_call(info, near, far, gain, w, parts):
    frames, lanes = len(near), near[0].shape[1]
    width, count = w.shape[1], frames * lanes
    return resident(
        functools.partial(time_cross_kernel, frames, parts),
        [
            ((D, count), jnp.bfloat16),
            ((8, count), jnp.float32),
            ((3, width, count), jnp.bfloat16),
        ],
        info,
        list(near) + list(far) + [gain, w],
        [],
        6 * D * width * count,
        12,
    )


def time_near_call(info, near, far, gain, w, crossed, parts, share):
    frames, lanes = len(near), near[0].shape[1]
    width, count = w.shape[1], frames * lanes
    return resident(
        functools.partial(time_near_kernel, frames, parts, share),
        [
            ((D, count), jnp.bfloat16),
            ((8, count), jnp.float32),
            ((width, 2 * count), jnp.bfloat16),
        ],
        info,
        list(near) + list(far) + [gain, w, crossed],
        [pltpu.VMEM((3, width, count), jnp.bfloat16)],
        6 * D * width * count,
        12,
    )


def time_far_call(info, sides, w, frames, share, keys, width):
    count = 2 * sides[0].shape[1]
    return resident(
        functools.partial(time_far_kernel, frames, share, keys, width),
        [((D - width, count), jnp.bfloat16)],
        info,
        list(sides) + list(w),
        [],
        6 * D * (D - width) * count,
        12,
    )[0]


def time_out_kernel(frames, parts, share, keys, first, info, *refs):
    near, refs = refs[:frames], refs[frames:]
    far, refs = refs[:frames], refs[frames:]
    att_near, att_far, o_own, refs = refs[0], refs[1], refs[2], refs[3:]
    o_far, (keep, send, ratios, att, res) = refs[: len(keys)], refs[len(keys) :]
    lanes = near[0].shape[1]
    width = o_own.shape[0]
    head_index, branch = place_of(HEADS), place_of(CFG)
    for r in range(parts):
        span = pl.ds(aligned(base_of(parts, r, width)), width)
        cols = slice(first * lanes, (first + frames) * lanes)
        att[span, :] = (
            att_near[:, cols] if r == 0 else att_far[(r - 1) * width : r * width, cols]
        )
    far_y = jnp.dot(
        jnp.concatenate([x[...] for x in o_far], axis=0),
        att[...],
        preferred_element_type=jnp.float32,
    )
    done = 0
    for key in [(0, 0, 0)] + list(keys):
        base = base_of(parts, key[0], width)
        if key[0]:
            count = o_far[keys.index(key)].shape[0]
            offset = quarter_of(key, count, *share)
            source, start = far, (key[0] - 1) * width + offset
            y = far_y[done : done + count]
            done += count
        else:
            count, offset, source, start = width, 0, near, 0
            y = jnp.dot(o_own[...], att[...], preferred_element_type=jnp.float32)
        for f in range(frames):
            if key[0]:
                x = source[f][pl.ds(aligned(start), count), :]
            else:
                x = source[f][0:count, :]
            x = x.astype(jnp.float32) + y[:, f * lanes : (f + 1) * lanes]
            res[f, pl.ds(aligned(base + offset), count), :] = x.astype(jnp.bfloat16)
    slot = keep.shape[2]
    for f in range(frames):
        tail = near[f][width:, :].astype(jnp.float32)
        ratios[f : f + 1, :] = tail[0:1] / tail[1:2]
        for r in range(parts):
            head = lax.rem(head_index + r, parts)
            keep[f, r] = res[f, pl.ds(aligned((head * 2 + branch) * slot), slot), :]
            send[f, r] = res[f, pl.ds(aligned((head * 2 + 1 - branch) * slot), slot), :]


def time_out_call(
    info, near, far, att_near, att_far, o_own, o_far, parts, share, keys, first
):
    frames, lanes = len(near), near[0].shape[1]
    result = ((frames, parts, D // (2 * parts), lanes), jnp.bfloat16)
    return resident(
        functools.partial(time_out_kernel, frames, parts, share, keys, first),
        [result, result, ((frames, lanes), jnp.float32)],
        info,
        list(near) + list(far) + [att_near, att_far, o_own] + list(o_far),
        [
            pltpu.VMEM((D, frames * lanes), jnp.bfloat16),
            pltpu.VMEM((frames, D, lanes), jnp.bfloat16),
        ],
        2 * D * D * frames * lanes,
        12,
    )


def guide_kernel(info, keep, other, ratios, *outs):
    frames, parts = keep.shape[0], keep.shape[1]
    branch = place_of(CFG)
    for f in range(frames):
        ratio = ratios[f : f + 1, :]
        for r in range(parts):
            mine = keep[f, r].astype(jnp.float32)
            theirs = other[f, r].astype(jnp.float32)
            cond = jnp.where(branch == 0, mine, theirs)
            uncond = jnp.where(branch == 0, theirs, mine)
            outs[f * parts + r][...] = (uncond + ratio * (cond - uncond)).astype(jnp.bfloat16)


def place_kernel(seq, parts, *refs):
    pieces, out, sems = refs[:-2], refs[-2], refs[-1]
    head, frame = place_of(HEADS), place_of(SEQ)
    half = seq // 2
    copies = []
    for i, (cross, m) in enumerate(roads(seq)):
        side = crossing(seq, cross) * half + lax.rem(lax.rem(frame, half) + m, half)
        for r in range(parts):
            piece = pieces[i * parts + r]
            slot = lax.rem(head - r + parts, parts) * seq + side
            lanes = piece.shape[1]
            view = out.at[:, pl.ds(aligned(slot * lanes, LANES), lanes)]
            copies.append(pltpu.make_async_copy(piece, view, sems.at[i * parts + r]))
    for copy in copies:
        copy.start()
    for copy in copies:
        copy.wait()


def place_call(pieces, seq, parts):
    rows, lanes = pieces[0].shape
    n = len(pieces)
    return pl.pallas_call(
        functools.partial(place_kernel, seq, parts),
        out_shape=jax.ShapeDtypeStruct((rows, n * lanes), jnp.bfloat16),
        in_specs=[pl.BlockSpec(memory_space=pltpu.VMEM)] * n,
        out_specs=pl.BlockSpec(memory_space=pltpu.HBM),
        scratch_shapes=[pltpu.SemaphoreType.DMA((n,))],
        compiler_params=pltpu.CompilerParams(vmem_limit_bytes=4 << 20),
    )(*[local(x) for x in pieces])


def split_kernel(seq, parts, source, *refs):
    outs, sems = refs[:-1], refs[-1]
    copies = []
    for i, out in enumerate(outs):
        block = out.shape[1]
        start = ((i % parts) * 2 + crossing(seq, i < parts)) * block
        view = source.at[:, pl.ds(aligned(start, LANES), block)]
        copies.append(pltpu.make_async_copy(view, out, sems.at[i]))
    for copy in copies:
        copy.start()
    for copy in copies:
        copy.wait()


def pick_kernel(share, w_out, w_time, w_last, w_space, gains, *refs):
    outs, w_here, column, sems = refs[:-3], refs[-3], refs[-2], refs[-1]
    rows = outs[-1].shape[0]
    start = quarter_of((0, 0, 0), rows, *share)
    inner = start + lax.rem(place_of(SEQ), 2) * outs[0].shape[0]
    moves = [
        (w_out, inner, outs[0]),
        (w_time.at[0], inner, outs[1]),
        (w_time.at[1], start, outs[2].at[0:rows, :]),
        (w_time.at[2], start, outs[2].at[rows:, :]),
        (w_last, start, outs[3]),
        (w_space, None, w_here),
    ]
    copies = []
    for i, (source, first, out) in enumerate(moves):
        view = source if first is None else source.at[pl.ds(aligned(first, 8), out.shape[0]), :]
        copies.append(pltpu.make_async_copy(view, out, sems.at[i]))
    for copy in copies:
        copy.start()
    row = lax.broadcasted_iota(jnp.int32, (LANES, LANES), 0)
    diagonal = row == lax.broadcasted_iota(jnp.int32, (LANES, LANES), 1)
    for i in range(gains.shape[0]):
        wide = jnp.broadcast_to(gains[i : i + 1, :].astype(jnp.float32), (LANES, LANES))
        column[i * LANES : (i + 1) * LANES, :] = jnp.sum(
            jnp.where(diagonal, wide, 0.0), axis=1, keepdims=True
        )
    for copy in copies:
        copy.wait()


def stack_kernel(own, other, out, sems):
    rows = own.shape[0]
    side = lax.rem(place_of(SEQ), 2)
    copies = [
        pltpu.make_async_copy(own, out.at[pl.ds(aligned(side * rows, 8), rows), :], sems.at[0]),
        pltpu.make_async_copy(
            other, out.at[pl.ds(aligned((1 - side) * rows, 8), rows), :], sems.at[1]
        ),
    ]
    for copy in copies:
        copy.start()
    for copy in copies:
        copy.wait()


def stack_call(own, other):
    rows, columns = own.shape
    place = pl.BlockSpec(memory_space=pltpu.VMEM)
    return pl.pallas_call(
        stack_kernel,
        out_shape=pltpu.VMEM((2 * rows, columns), own.dtype),
        in_specs=[place, place],
        out_specs=place,
        scratch_shapes=[pltpu.SemaphoreType.DMA((2,))],
        compiler_params=pltpu.CompilerParams(vmem_limit_bytes=2 << 20),
    )(local(own), local(other))


def roads(seq):
    return [(cross, m) for cross in (0, 1) for m in range(seq // 2)]


def follow(seq, road, i, back=False):
    cross, m = road
    half = seq // 2
    side = i // half
    return (1 - side if cross else side) * half + (i % half + (-m if back else m)) % half


def shift(x, axis, by):
    size = lax.axis_size(axis)
    return lax.ppermute(x, axis, [(i, (i + by) % size) for i in range(size)])


def after(x, *gates):
    return lax.optimization_barrier((x,) + gates)[0]


def shards(fit, *args):
    (video_tokens, _, _, _, _, _, _, _, _, _, _) = args
    heads, seq = lax.axis_size(HEADS), lax.axis_size(SEQ)
    positions = video_tokens.shape[3]
    lanes = positions // (heads * seq)
    if not fit or lanes % LANES or seq % 4 or video_tokens.shape[1] != 1:
        return shards_plain(*args)
    return shards_fast(*args)


def shards_fast(
    video_tokens,
    text_tokens,
    text_length,
    guide_numer,
    guide_denom,
    spatial_gain,
    spatial_qkv,
    spatial_out,
    temporal_gain,
    temporal_qkv,
    temporal_out,
):
    heads, seq = lax.axis_size(HEADS), lax.axis_size(SEQ)
    groups, cfg = lax.axis_size(GROUPS), lax.axis_size(CFG)
    positions = video_tokens.shape[3]
    lanes = positions // (heads * seq)
    video, text = video_tokens[0, 0], text_tokens[0, 0]
    width = video.shape[0]
    rows = width // (groups * cfg)
    per = 2
    block = positions // (heads * per)
    ring = range(1, heads)
    info = jnp.concatenate([text_length[0], guide_numer, guide_denom])
    gains = jnp.concatenate([spatial_gain, temporal_gain]).reshape(-1, LANES)

    text_set = [text] + [shift(text, HEADS, r) for r in ring]
    parts = pl.pallas_call(
        functools.partial(split_kernel, seq, heads),
        out_shape=(jax.ShapeDtypeStruct((width, block), jnp.bfloat16),) * (heads * per),
        in_specs=[pl.BlockSpec(memory_space=pltpu.HBM)],
        out_specs=(pl.BlockSpec(memory_space=pltpu.VMEM),) * (heads * per),
        scratch_shapes=[pltpu.SemaphoreType.DMA((heads * per,))],
        compiler_params=pltpu.CompilerParams(vmem_limit_bytes=8 << 20),
    )(pltpu.with_memory_space_constraint(video, pltpu.HBM))
    chunk_sets = []
    for part in parts:
        chunk_sets.append([part] + [shift(part, HEADS, r) for r in ring])

    sources = [
        pltpu.with_memory_space_constraint(x, pltpu.HBM)
        for x in (spatial_out, temporal_qkv, temporal_out, spatial_qkv)
    ]
    whole, part = (rows, D), (rows // 2, D)
    *mine, spatial_here, gain = pl.pallas_call(
        functools.partial(pick_kernel, (groups, cfg)),
        out_shape=tuple(
            jax.ShapeDtypeStruct(shape, jnp.bfloat16)
            for shape in (part, part, (2 * rows, D), whole)
        )
        + (
            pltpu.VMEM(spatial_qkv.shape, jnp.bfloat16),
            pltpu.VMEM((2 * D, 1), jnp.float32),
        ),
        in_specs=[pl.BlockSpec(memory_space=pltpu.HBM)] * 4
        + [pl.BlockSpec(memory_space=pltpu.VMEM)],
        out_specs=(pl.BlockSpec(memory_space=pltpu.VMEM),) * 6,
        scratch_shapes=[pltpu.SemaphoreType.DMA((6,))],
        compiler_params=pltpu.CompilerParams(vmem_limit_bytes=12 << 20),
    )(*sources, gains)

    chunks = []
    mark, states = None, []
    aheads = list(range(1, heads)) + [0]
    for j, chunk in enumerate(chunk_sets):
        if j == 0:
            text_kv, made = project_call(
                info, [text_set, chunk], [(1, 2), (0, 1, 2)], gain, spatial_here
            )
        else:
            ready = [chunk[0]] + [after(x, mark) for x in chunk[1:]]
            (made,) = project_call(info, [ready], [(0, 1, 2)], gain, spatial_here)
        chunks.append(made)
        mark = made
        if heads - 1 <= j < heads * per - 1:
            fresh = chunks if j == heads - 1 else [made]
            states = attend_call(
                info,
                chunks[:heads],
                fresh,
                text_kv if j == heads - 1 else None,
                states,
                aheads,
                False,
            )
            mark = states[0]

    keys = [(r, dg, dc) for r in ring for dg in range(groups) for dc in range(cfg)]

    def first_hop(w, gate=None):
        w = w if gate is None else after(w, gate)
        return {(r, 0, 0): shift(w, HEADS, r) for r in ring}

    def trade(held, gate):
        pairs = [(i, i ^ 1) for i in range(seq)]
        for r in ring:
            own = after(held[r, 0, 0], gate)
            held[r, 0, 0] = own, lax.ppermute(own, SEQ, pairs)

    def join(held, gate):
        for r in ring:
            own, other = held[r, 0, 0]
            held[r, 0, 0] = stack_call(own, after(other, gate))

    def second_hop(held, gate):
        for r in ring:
            for dg in range(1, groups):
                source = after(held[r, 0, 0], gate)
                held[r, dg, 0] = shift(source, GROUPS, dg)

    def third_hop(held, gate):
        for r in ring:
            for dg in range(groups):
                for dc in range(1, cfg):
                    source = after(held[r, dg, 0], gate)
                    held[r, dg, dc] = shift(source, CFG, dc)

    far_out = first_hop(mine[0])
    far_time = [first_hop(mine[1])]
    att = {}

    def attend(cross, r):
        if cross:
            n = aheads.index(r)
            state = states[2 * n : 2 * n + 2]
            return attend_call(info, chunks[:heads], chunks[-1:], None, state, [r], True)[0]
        return attend_call(info, chunks[heads:], chunks, text_kv, [], [r], True)[0]

    def attend_far(cross):
        for r in ring:
            mark = attend(cross, r)
            att[cross, r] = shift(mark, HEADS, r)
        return mark

    def held_tokens(r, cross):
        return [x[r] for x in (chunk_sets[:heads] if cross else chunk_sets[heads:])]

    split = (groups, cfg)
    near, far = {}, {}

    def out_rows(cross, own, others):
        att_all = [att[cross, r] for r in range(heads)]
        part = [(0, 0, 0)] * own + keys * others
        got = out_call(
            info,
            att_all,
            [held_tokens(key[0], cross) for key in part],
            [far_out[key] if key[0] else spatial_out for key in part],
            16 * own,
            seq,
            part,
            split,
        )
        if own:
            near.update({(cross, m): got[m] for m in range(seq // 2)})
        if others:
            far.update({(cross, m): got[m + seq // 2 * own] for m in range(seq // 2)})
        return got[0]

    first = attend_far(1)
    trade(far_out, first)
    att[1, 0] = attend(1, 0)
    trade(far_time[0], att[1, 0])
    join(far_out, att[1, 0])
    second_hop(far_out, att[1, 0])
    early = out_rows(1, 1, 0)
    join(far_time[0], early)
    third_hop(far_out, early)
    second = attend_far(0)
    middle = out_rows(1, 0, 1)
    att[0, 0] = attend(0, 0)
    late = out_rows(0, 1, 1)
    far_time.append(first_hop(mine[2], first))
    far_last = first_hop(mine[3], second)
    for held, gate in zip(far_time, (early, second)):
        second_hop(held, gate)
        third_hop(held, late)

    def send_all(held):
        moved = []
        for road in roads(seq):
            x = held[road]
            if road != (0, 0):
                route = [(i, follow(seq, road, i)) for i in range(seq)]
                x = lax.ppermute(x, SEQ, route)
            moved.append(x)
        return moved

    near, far = send_all(near), send_all(far)
    second_hop(far_last, far[seq // 2])
    third_hop(far_last, far[seq // 2])
    share = groups * cfg
    mid = seq // 2
    xs_cross, inverse_cross, crossed = time_cross_call(
        info, near[mid:], far[mid:], gain, temporal_qkv, heads
    )
    xs, inverse, att_near = time_near_call(
        info, near[:mid], far[:mid], gain, temporal_qkv, crossed, heads, share
    )
    att_far = time_far_call(
        info,
        [xs, inverse, xs_cross, inverse_cross],
        [far_time[kind][key] for key in keys for kind in range(2)],
        seq,
        split,
        keys,
        width,
    )
    slot = D // (heads * cfg)
    landed = {}
    results = {}
    for cross in (1, 0):
        picked = [i for i, road in enumerate(roads(seq)) if road[0] == cross]
        keep, send, ratios = time_out_call(
            info,
            [near[i] for i in picked],
            [far[i] for i in picked],
            att_near,
            att_far,
            temporal_out,
            [far_last[key] for key in keys],
            heads,
            split,
            keys,
            picked[0],
        )
        results[cross] = keep, shift(send, CFG, 1), ratios
    for cross in (1, 0):
        picked = [i for i, road in enumerate(roads(seq)) if road[0] == cross]
        pieces = resident(
            guide_kernel,
            [((slot, lanes), jnp.bfloat16)] * (len(picked) * heads),
            info,
            results[cross],
            [],
            len(picked) * D * lanes,
            8,
        )
        for n, i in enumerate(picked):
            road = roads(seq)[i]
            for r in range(heads):
                piece = pieces[n * heads + r]
                if road != (0, 0) or r:
                    route = [
                        (a * heads + b, follow(seq, road, a, True) * heads + (b + r) % heads)
                        for a in range(seq)
                        for b in range(heads)
                    ]
                    piece = lax.ppermute(piece, (SEQ, HEADS), route)
                landed[i, r] = piece
    landed = [landed[i, r] for i in range(seq) for r in range(heads)]
    result = place_call(landed, seq, heads)
    return result[None]


def solution(mesh):
    return jax.shard_map(
        functools.partial(shards, fits(mesh)),
        mesh=mesh,
        in_specs=(
            P(CFG, (GROUPS, SEQ), HEADS, None),
            P(CFG, (GROUPS, SEQ), HEADS, None),
            P(CFG, (GROUPS, SEQ)),
            P((GROUPS, SEQ)),
            P((GROUPS, SEQ)),
            P(),
            P(None, HEADS, None),
            P(HEADS, None),
            P(),
            P(None, HEADS, None),
            P(HEADS, None),
        ),
        out_specs=P((GROUPS, SEQ), (HEADS, CFG), None),
        check_vma=False,
    )
```

profile of v0, /device:TPU:0, one launch (start us, length us, event | category | flops | bytes accessed | tf_op | source)
XLA Modules:
  0.0 155.0 jit_solution(14647403343214991595)
XLA Ops:
  1.3 3.0 %collective-permute-start.2 = (bf16[576,256]{1,0:T(8,128)(2,1)S(1)}, bf16[576,256]{1,0:T(8,128)(2,1)S(1)}, u32[]{:S(2)}, u32[]{:S(2)}) collective-permute-start(bf16[576,256]{1,0:T(8,128)(2,1)S(1)} %get-tuple-element.74.refs_2_), channel_id=1, source_target_pairs={{0,2},{2,0},{1,3},{3,1},{4,6},{6,4},{5,7},{7,5},{8,10},{10,8},{9,1... | collective-permute-start | bytes 884744 | tf_op jit(solution)/shard_map/ppermute | solution.py:773
  4.4 1.9 %collective-permute-start.3 = (bf16[576,256]{1,0:T(8,128)(2,1)S(1)}, bf16[576,256]{1,0:T(8,128)(2,1)S(1)}, u32[]{:S(2)}, u32[]{:S(2)}) collective-permute-start(bf16[576,256]{1,0:T(8,128)(2,1)S(1)} %get-tuple-element.78.refs_0_.refs_3_), channel_id=1, source_target_pairs={{0,2},{2,0},{1,3},{3,1},{4,6},{6,4},{5,7},{7,5},{8,10},{10,8},{9,1... | collective-permute-start | bytes 884744 | tf_op jit(solution)/shard_map/ppermute | solution.py:773
  6.4 1.9 %collective-permute-start.4 = (bf16[576,256]{1,0:T(8,128)(2,1)S(1)}, bf16[576,256]{1,0:T(8,128)(2,1)S(1)}, u32[]{:S(2)}, u32[]{:S(2)}) collective-permute-start(bf16[576,256]{1,0:T(8,128)(2,1)S(1)} %get-tuple-element.83.refs_0_.refs_3_), channel_id=1, source_target_pairs={{0,2},{2,0},{1,3},{3,1},{4,6},{6,4},{5,7},{7,5},{8,10},{10,8},{9,1... | collective-permute-start | bytes 884744 | tf_op jit(solution)/shard_map/ppermute | solution.py:773
  11.0 2.9 %shard_map.110 = (bf16[72,1152]{1,0:T(8,128)(2,1)S(1)}, bf16[72,1152]{1,0:T(8,128)(2,1)S(1)}, bf16[288,1152]{1,0:T(8,128)(2,1)S(1)}, bf16[144,1152]{1,0:T(8,128)...) custom-call(bf16[576,1152]{1,0:T(8,128)(2,1)} %refs_12_.1, bf16[3,576,1152]{2,1,0:T(8,128)(2,1)} %refs_5_.3, ...), custom_call_target="tpu_custom_call" | custom-call | tf_op jit(solution)/shard_map/pallas_call | solution.py:834
  14.0 1.3 collective-permute-done.1.refs_1_
  15.3 2.8 %shard_map.111 = (bf16[2,8,80,128]{3,2,1,0:T(8,128)(2,1)S(1)}, bf16[3,8,80,256]{3,2,1,0:T(8,128)(2,1)S(1)}) custom-call(s32[3]{0:T(128)S(1)} %pad_add_fusion.info, bf16[576,128]{1,0:T(8,128)(2,1)S(1)} %bitcast.8, bf16[576,128]{1,0:T(8,128)(2,1)S(1)} %collective-permute-done.1.refs_1_, bf16[576,256]{1,0:T(8,128)(2,1)S(1)} %get-tuple-element.74.refs_2_, ...), custom_call_target="tpu_custom_call" | custom-call | flops 1528823808 | bytes 4875264 | tf_op jit(solution)/shard_map/pallas_call | solution.py:161
  18.2 3.5 %collective-permute-done.3.refs_1_.refs_3_.refs_5_.refs_7_.refs_9_ = bf16[576,256]{1,0:T(8,128)(2,1)S(1)} collective-permute-done((bf16[576,256]{1,0:T(8,128)(2,1)S(1)}, bf16[576,256]{1,0:T(8,128)(2,1)S(1)}, u32[]{:S(2)}, u32[]{:S(2)}) %collective-permute-start.3) | collective-permute-done | bytes 294944 | tf_op jit(solution)/shard_map/ppermute | solution.py:773
  21.7 2.1 %shard_map.112.refs_1_.refs_3_ = bf16[3,8,80,256]{3,2,1,0:T(8,128)(2,1)S(1)} custom-call(s32[3]{0:T(128)S(1)} %pad_add_fusion.info, bf16[576,256]{1,0:T(8,128)(2,1)S(1)} %get-tuple-element.78.refs_0_.refs_3_, bf16[576,256]{1,0:T(8,128)(2,1)S(1)} %collective-permute-done.3.refs_1_.refs_3_.refs_5_.refs_7_.refs_9_, ...), custom_call_target="tpu_custom_call" | custom-call | flops 1019215872 | bytes 4580352 | tf_op jit(solution)/shard_map/pallas_call | solution.py:161
  23.8 4.1 %shard_map.113 = (f32[8,80,256]{2,1,0:T(8,128)S(1)}, f32[8,8,256]{2,1,0:T(8,128)S(1)}, f32[8,80,256]{2,1,0:T(8,128)S(1)}, f32[8,8,256]{2,1,0:T(8,128)S(1)}) custom-call(s32[3]{0:T(128)S(1)} %pad_add_fusion.info, bf16[3,8,80,256]{3,2,1,0:T(8,128)(2,1)S(1)} %get-tuple-element.77.refs_0_.refs_2_, bf16[3,8,80,256]{3,2,1,0:T(8,128)(2,1)S(1)} %shard_map.112.refs_1_.refs_3_, ...), custom_call_target="tpu_custom_call" | custom-call | flops 2684354560 | bytes 4259840 | tf_op jit(solution)/shard_map/pallas_call | solution.py:161
  28.0 2.1 %shard_map.114.refs_2_.refs_0_.refs_4_ = bf16[3,8,80,256]{3,2,1,0:T(8,128)(2,1)S(1)} custom-call(s32[3]{0:T(128)S(1)} %pad_add_fusion.info, bf16[576,256]{1,0:T(8,128)(2,1)S(1)} %get-tuple-element.73.refs_0_.refs_2_, bf16[576,256]{1,0:T(8,128)(2,1)S(1)} %collective-permute-done.refs_1_.refs_4_.refs_6_.refs_8_.refs_10_, ...), custom_call_target="tpu_custom_call" | custom-call | flops 1019215872 | bytes 4580352 | tf_op jit(solution)/shard_map/pallas_call | solution.py:161
  30.1 2.0 %shard_map.115 = (f32[8,80,256]{2,1,0:T(8,128)S(1)}, f32[8,8,256]{2,1,0:T(8,128)S(1)}, f32[8,80,256]{2,1,0:T(8,128)S(1)}, f32[8,8,256]{2,1,0:T(8,128)S(1)}) custom-call(s32[3]{0:T(128)S(1)} %pad_add_fusion.info, bf16[3,8,80,256]{3,2,1,0:T(8,128)(2,1)S(1)} %get-tuple-element.77.refs_0_.refs_2_, bf16[3,8,80,256]{3,2,1,0:T(8,128)(2,1)S(1)} %shard_map.112.refs_1_.refs_3_, ...), custom_call_target="tpu_custom_call" | custom-call | flops 1073741824 | bytes 4390912 | tf_op jit(solution)/shard_map/pallas_call | solution.py:161
  32.1 1.3 collective-permute-done.4.refs_1_.refs_5_.refs_7_.refs_9_.refs_11_
  33.4 2.1 %shard_map.116.refs_1_.refs_5_.refs_2_ = bf16[3,8,80,256]{3,2,1,0:T(8,128)(2,1)S(1)} custom-call(s32[3]{0:T(128)S(1)} %pad_add_fusion.info, bf16[576,256]{1,0:T(8,128)(2,1)S(1)} %get-tuple-element.83.refs_0_.refs_3_, bf16[576,256]{1,0:T(8,128)(2,1)S(1)} %collective-permute-done.4.refs_1_.refs_5_.refs_7_.refs_9_.refs_11_, ...), custom_call_target="tpu_custom_call" | custom-call | flops 1019215872 | bytes 4580352 | tf_op jit(solution)/shard_map/pallas_call | solution.py:161
  35.6 1.5 shard_map.119
  37.1 1.8 %collective-permute-start.20 = (bf16[288,1152]{1,0:T(8,128)(2,1)S(1)}, bf16[288,1152]{1,0:T(8,128)(2,1)S(1)}, u32[]{:S(2)}, u32[]{:S(2)}) collective-permute-start(bf16[288,1152]{1,0:T(8,128)(2,1)S(1)} %get-tuple-element.116), channel_id=1, source_target_pairs={{0,2},{2,0},{1,3},{3,1},{4,6},{6,4},{5,7},{7,5},{8,10},{10,8},{9,1... | collective-permute-start | bytes 1990664 | tf_op jit(solution)/shard_map/ppermute | solution.py:773
  39.2 17.6 %collective-permute-done.6.own = bf16[72,1152]{1,0:T(8,128)(2,1)S(1)} collective-permute-done((bf16[72,1152]{1,0:T(8,128)(2,1)S(1)}, bf16[72,1152]{1,0:T(8,128)(2,1)S(1)}, u32[]{:S(2)}, u32[]{:S(2)}) %collective-permute-start.6) | collective-permute-done | bytes 165920 | tf_op jit(solution)/shard_map/ppermute | solution.py:773
  56.8 1.5 collective-permute-start.7
  58.3 1.5 shard_map.120.refs_0_
  59.9 2.3 %collective-permute-done.7.other = bf16[72,1152]{1,0:T(8,128)(2,1)S(1)} collective-permute-done((bf16[72,1152]{1,0:T(8,128)(2,1)S(1)}, bf16[72,1152]{1,0:T(8,128)(2,1)S(1)}, u32[]{:S(2)}, u32[]{:S(2)}) %collective-permute-start.7) | collective-permute-done | bytes 165920 | tf_op jit(solution)/shard_map/ppermute | solution.py:887
  62.5 1.6 %collective-permute-start.10 = (bf16[144,1152]{1,0:T(8,128)(2,1)S(1)}, bf16[144,1152]{1,0:T(8,128)(2,1)S(1)}, u32[]{:S(2)}, u32[]{:S(2)}) collective-permute-start(bf16[144,1152]{1,0:T(8,128)(2,1)S(1)} %shard_map.121.refs_13_.refs_10_), channel_id=1, source_target_pairs={{0,16},{16,0},{1,17},{17,1},{2,18},{18,2},{3,19},{19,3},{4,20},{20... | collective-permute-start | bytes 995336 | tf_op jit(solution)/shard_map/ppermute | solution.py:773
  64.1 1.5 collective-permute-start.8
  66.1 3.8 %shard_map.118 = bf16[576,256]{1,0:T(8,128)(2,1)S(1)} custom-call(s32[3]{0:T(128)S(1)} %pad_add_fusion.info, bf16[3,8,80,256]{3,2,1,0:T(8,128)(2,1)S(1)} %shard_map.114.refs_2_.refs_0_.refs_4_, bf16[3,8,80,256]{3,2,1,0:T(8,128)(2,1)S(1)} %shard_map.116.refs_1_.refs_5_.refs_2_, bf16[3,8,80,256]{3,2,1,0:T(8,128)(2,1)S(1)} %get-tuple-element.77.refs_0_.refs_2_, ...), custom_call_target="tpu_custom_call" | custom-call | flops 2415919104 | bytes 6225920 | tf_op jit(solution)/shard_map/pallas_call | solution.py:161
  73.3 1.5 collective-permute-start.5
  74.8 1.6 %collective-permute-start.19 = (bf16[72,1152]{1,0:T(8,128)(2,1)S(1)}, bf16[72,1152]{1,0:T(8,128)(2,1)S(1)}, u32[]{:S(2)}, u32[]{:S(2)}) collective-permute-start(bf16[72,1152]{1,0:T(8,128)(2,1)S(1)} %collective-permute-done.18.own), channel_id=1, source_target_pairs={{0,4},{4,0},{8,12},{12,8},{1,5},{5,1},{9,13},{13,9},{2,6},{6,2},{1... | collective-permute-start | bytes 497672 | tf_op jit(solution)/shard_map/ppermute | solution.py:887
  76.4 4.4 %collective-permute-done.19.other = bf16[72,1152]{1,0:T(8,128)(2,1)S(1)} collective-permute-done((bf16[72,1152]{1,0:T(8,128)(2,1)S(1)}, bf16[72,1152]{1,0:T(8,128)(2,1)S(1)}, u32[]{:S(2)}, u32[]{:S(2)}) %collective-permute-start.19) | collective-permute-done | bytes 165920 | tf_op jit(solution)/shard_map/ppermute | solution.py:887
  81.7 2.6 %collective-permute-start.14 = (bf16[592,128]{1,0:T(8,128)(2,1)S(1)}, bf16[592,128]{1,0:T(8,128)(2,1)S(1)}, u32[]{:S(2)}, u32[]{:S(2)}) collective-permute-start(bf16[592,128]{1,0:T(8,128)(2,1)S(1)} %get-tuple-element.95), channel_id=1, source_target_pairs={{0,8},{4,12},{8,0},{12,4},{1,9},{5,13},{9,1},{13,5},{2,10},{6,14},... | collective-permute-start | bytes 454664 | tf_op jit(solution)/shard_map/ppermute | solution.py:974
  86.8 4.0 %shard_map.117.refs_0_ = bf16[576,256]{1,0:T(8,128)(2,1)S(1)} custom-call(s32[3]{0:T(128)S(1)} %pad_add_fusion.info, bf16[3,8,80,256]{3,2,1,0:T(8,128)(2,1)S(1)} %shard_map.114.refs_2_.refs_0_.refs_4_, bf16[3,8,80,256]{3,2,1,0:T(8,128)(2,1)S(1)} %shard_map.116.refs_1_.refs_5_.refs_2_, bf16[3,8,80,256]{3,2,1,0:T(8,128)(2,1)S(1)} %get-tuple-element.77.refs_0_.refs_2_, ...), custom_call_target="tpu_custom_call" | custom-call | flops 2415919104 | bytes 6225920 | tf_op jit(solution)/shard_map/pallas_call | solution.py:161
  90.8 3.4 %collective-permute-start.15 = (bf16[592,128]{1,0:T(8,128)(2,1)S(1)}, bf16[592,128]{1,0:T(8,128)(2,1)S(1)}, u32[]{:S(2)}, u32[]{:S(2)}) collective-permute-start(bf16[592,128]{1,0:T(8,128)(2,1)S(1)} %get-tuple-element.103), channel_id=1, source_target_pairs={{0,12},{4,8},{8,4},{12,0},{1,13},{5,9},{9,5},{13,1},{2,14},{6,10},... | collective-permute-start | bytes 454664 | tf_op jit(solution)/shard_map/ppermute | solution.py:974
  94.2 1.6 %shard_map.123 = (bf16[592,128]{1,0:T(8,128)(2,1)S(1)}, bf16[592,128]{1,0:T(8,128)(2,1)S(1)}, bf16[576,128]{1,0:T(8,128)(2,1)S(1)}, bf16[576,128]{1,0:T(8,128)(2,1)S(1)}) custom-call(s32[3]{0:T(128)S(1)} %pad_add_fusion.info, bf16[576,256]{1,0:T(8,128)(2,1)S(1)} %shard_map.117.refs_0_, bf16[576,256]{1,0:T(8,128)(2,1)S(1)} %collective-permute-done.5.refs_1_, ...), custom_call_target="tpu_custom_call" | custom-call | flops 679477248 | bytes 6193152 | tf_op jit(solution)/shard_map/pallas_call | solution.py:161
  95.9 5.2 %collective-permute-done.16.refs_2_ = bf16[576,128]{1,0:T(8,128)(2,1)S(1)} collective-permute-done((bf16[576,128]{1,0:T(8,128)(2,1)S(1)}, bf16[576,128]{1,0:T(8,128)(2,1)S(1)}, u32[]{:S(2)}, u32[]{:S(2)}) %collective-permute-start.16) | collective-permute-done | bytes 147488 | tf_op jit(solution)/shard_map/ppermute | solution.py:974
  101.9 3.2 %collective-permute-start.17 = (bf16[576,128]{1,0:T(8,128)(2,1)S(1)}, bf16[576,128]{1,0:T(8,128)(2,1)S(1)}, u32[]{:S(2)}, u32[]{:S(2)}) collective-permute-start(bf16[576,128]{1,0:T(8,128)(2,1)S(1)} %get-tuple-element.105), channel_id=1, source_target_pairs={{0,12},{4,8},{8,4},{12,0},{1,13},{5,9},{9,5},{13,1},{2,14},{6,10},... | collective-permute-start | bytes 442376 | tf_op jit(solution)/shard_map/ppermute | solution.py:974
  105.1 4.8 %collective-permute-done.17.refs_3_ = bf16[576,128]{1,0:T(8,128)(2,1)S(1)} collective-permute-done((bf16[576,128]{1,0:T(8,128)(2,1)S(1)}, bf16[576,128]{1,0:T(8,128)(2,1)S(1)}, u32[]{:S(2)}, u32[]{:S(2)}) %collective-permute-start.17) | collective-permute-done | bytes 147488 | tf_op jit(solution)/shard_map/ppermute | solution.py:974
  109.9 1.6 %collective-permute-start.13 = (bf16[576,128]{1,0:T(8,128)(2,1)S(1)}, bf16[576,128]{1,0:T(8,128)(2,1)S(1)}, u32[]{:S(2)}, u32[]{:S(2)}) collective-permute-start(bf16[576,128]{1,0:T(8,128)(2,1)S(1)} %get-tuple-element.102), channel_id=1, source_target_pairs={{0,4},{4,0},{8,12},{12,8},{1,5},{5,1},{9,13},{13,9},{2,6},{6,2},{1... | collective-permute-start | bytes 442376 | tf_op jit(solution)/shard_map/ppermute | solution.py:974
  111.5 3.5 %collective-permute-done.13.refs_3_ = bf16[576,128]{1,0:T(8,128)(2,1)S(1)} collective-permute-done((bf16[576,128]{1,0:T(8,128)(2,1)S(1)}, bf16[576,128]{1,0:T(8,128)(2,1)S(1)}, u32[]{:S(2)}, u32[]{:S(2)}) %collective-permute-start.13) | collective-permute-done | bytes 147488 | tf_op jit(solution)/shard_map/ppermute | solution.py:974
  115.0 1.6 %collective-permute-start.12 = (bf16[592,128]{1,0:T(8,128)(2,1)S(1)}, bf16[592,128]{1,0:T(8,128)(2,1)S(1)}, u32[]{:S(2)}, u32[]{:S(2)}) collective-permute-start(bf16[592,128]{1,0:T(8,128)(2,1)S(1)} %get-tuple-element.100), channel_id=1, source_target_pairs={{0,4},{4,0},{8,12},{12,8},{1,5},{5,1},{9,13},{13,9},{2,6},{6,2},{1... | collective-permute-start | bytes 454664 | tf_op jit(solution)/shard_map/ppermute | solution.py:974
  116.6 3.6 %collective-permute-done.12.refs_1_ = bf16[592,128]{1,0:T(8,128)(2,1)S(1)} collective-permute-done((bf16[592,128]{1,0:T(8,128)(2,1)S(1)}, bf16[592,128]{1,0:T(8,128)(2,1)S(1)}, u32[]{:S(2)}, u32[]{:S(2)}) %collective-permute-start.12) | collective-permute-done | bytes 151584 | tf_op jit(solution)/shard_map/ppermute | solution.py:974
  120.7 2.2 %shard_map.125 = (bf16[1152,256]{1,0:T(8,128)(2,1)S(1)}, f32[8,256]{1,0:T(8,128)S(1)}, bf16[3,576,256]{2,1,0:T(8,128)(2,1)S(1)}) custom-call(s32[3]{0:T(128)S(1)} %pad_add_fusion.info, bf16[592,128]{1,0:T(8,128)(2,1)S(1)} %collective-permute-done.14.refs_0_, bf16[592,128]{1,0:T(8,128)(2,1)S(1)} %collective-permute-done.15.refs_1_, ...), custom_call_target="tpu_custom_call" | custom-call | flops 1019215872 | bytes 4588544 | tf_op jit(solution)/shard_map/pallas_call | solution.py:161
  122.9 2.8 %shard_map.126 = (bf16[1152,256]{1,0:T(8,128)(2,1)S(1)}, f32[8,256]{1,0:T(8,128)S(1)}, bf16[576,512]{1,0:T(8,128)(2,1)S(1)}) custom-call(s32[3]{0:T(128)S(1)} %pad_add_fusion.info, bf16[592,128]{1,0:T(8,128)(2,1)S(1)} %get-tuple-element.99.refs_0_, bf16[592,128]{1,0:T(8,128)(2,1)S(1)} %collective-permute-done.12.refs_1_, ...), custom_call_target="tpu_custom_call" | custom-call | flops 1019215872 | bytes 5473280 | tf_op jit(solution)/shard_map/pallas_call | solution.py:161
  125.8 3.6 %shard_map.128.refs_5_ = bf16[576,512]{1,0:T(8,128)(2,1)S(1)} custom-call(s32[3]{0:T(128)S(1)} %pad_add_fusion.info, bf16[1152,256]{1,0:T(8,128)(2,1)S(1)} %get-tuple-element.108.refs_0_, f32[8,256]{1,0:T(8,128)S(1)} %get-tuple-element.109.refs_1_, bf16[1152,256]{1,0:T(8,128)(2,1)S(1)} %get-tuple-element.110.refs_2_, ...), custom_call_target="tpu_custom_call" | custom-call | flops 2038431744 | bytes 5177344 | tf_op jit(solution)/shard_map/pallas_call | solution.py:161
  129.4 1.6 %shard_map.131 = (bf16[2,2,288,128]{3,2,1,0:T(8,128)(2,1)S(1)}, bf16[2,2,288,128]{3,2,1,0:T(8,128)(2,1)S(1)}, f32[2,128]{1,0:T(2,128)S(1)}) custom-call(s32[3]{0:T(128)S(1)} %pad_add_fusion.info, bf16[592,128]{1,0:T(8,128)(2,1)S(1)} %collective-permute-done.14.refs_0_, bf16[592,128]{1,0:T(8,128)(2,1)S(1)} %collective-permute-done.15.refs_1_, ...), custom_call_target="tpu_custom_call" | custom-call | flops 679477248 | bytes 4431872 | tf_op jit(solution)/shard_map/pallas_call | solution.py:161
  131.1 1.6 %shard_map.129 = (bf16[2,2,288,128]{3,2,1,0:T(8,128)(2,1)S(1)}, bf16[2,2,288,128]{3,2,1,0:T(8,128)(2,1)S(1)}, f32[2,128]{1,0:T(2,128)S(1)}) custom-call(s32[3]{0:T(128)S(1)} %pad_add_fusion.info, bf16[592,128]{1,0:T(8,128)(2,1)S(1)} %get-tuple-element.99.refs_0_, bf16[592,128]{1,0:T(8,128)(2,1)S(1)} %collective-permute-done.12.refs_1_, ...), custom_call_target="tpu_custom_call" | custom-call | flops 679477248 | bytes 4431872 | tf_op jit(solution)/shard_map/pallas_call | solution.py:161
  133.9 2.4 %collective-permute-start.36 = (bf16[288,128]{1,0:T(8,128)(2,1)S(1)}, bf16[288,128]{1,0:T(8,128)(2,1)S(1)}, u32[]{:S(2)}, u32[]{:S(2)}) collective-permute-start(bf16[288,128]{1,0:T(8,128)(2,1)S(1)} %get-tuple-element.137), channel_id=1, source_target_pairs={{0,8},{2,10},{4,12},{6,14},{8,0},{10,2},{12,4},{14,6},{1,9},{3,11}... | collective-permute-start | bytes 221192 | tf_op jit(solution)/shard_map/ppermute | solution.py:1038
  136.3 1.6 %collective-permute-start.37 = (bf16[288,128]{1,0:T(8,128)(2,1)S(1)}, bf16[288,128]{1,0:T(8,128)(2,1)S(1)}, u32[]{:S(2)}, u32[]{:S(2)}) collective-permute-start(bf16[288,128]{1,0:T(8,128)(2,1)S(1)} %get-tuple-element.138), channel_id=1, source_target_pairs={{0,10},{2,8},{4,14},{6,12},{8,2},{10,0},{12,6},{14,4},{1,11},{3,9}... | collective-permute-start | bytes 221192 | tf_op jit(solution)/shard_map/ppermute | solution.py:1038
  137.9 3.2 %collective-permute-start.38 = (bf16[288,128]{1,0:T(8,128)(2,1)S(1)}, bf16[288,128]{1,0:T(8,128)(2,1)S(1)}, u32[]{:S(2)}, u32[]{:S(2)}) collective-permute-start(bf16[288,128]{1,0:T(8,128)(2,1)S(1)} %get-tuple-element.139), channel_id=1, source_target_pairs={{0,12},{2,14},{4,8},{6,10},{8,4},{10,6},{12,0},{14,2},{1,13},{3,15... | collective-permute-start | bytes 221192 | tf_op jit(solution)/shard_map/ppermute | solution.py:1038
  142.4 1.6 %collective-permute-start.32 = (bf16[288,128]{1,0:T(8,128)(2,1)S(1)}, bf16[288,128]{1,0:T(8,128)(2,1)S(1)}, u32[]{:S(2)}, u32[]{:S(2)}) collective-permute-start(bf16[288,128]{1,0:T(8,128)(2,1)S(1)} %get-tuple-element.131), channel_id=1, source_target_pairs={{0,2},{2,0},{4,6},{6,4},{8,10},{10,8},{12,14},{14,12},{1,3},{3,1},... | collective-permute-start | bytes 221192 | tf_op jit(solution)/shard_map/ppermute | solution.py:1038
  144.0 1.3 collective-permute-start.33
  145.3 3.4 %collective-permute-done.37.refs_5_ = bf16[288,128]{1,0:T(8,128)(2,1)S(1)} collective-permute-done((bf16[288,128]{1,0:T(8,128)(2,1)S(1)}, bf16[288,128]{1,0:T(8,128)(2,1)S(1)}, u32[]{:S(2)}, u32[]{:S(2)}) %collective-permute-start.37) | collective-permute-done | bytes 73760 | tf_op jit(solution)/shard_map/ppermute | solution.py:1038
  148.9 5.0 %collective-permute-done.34.refs_3_ = bf16[288,128]{1,0:T(8,128)(2,1)S(1)} collective-permute-done((bf16[288,128]{1,0:T(8,128)(2,1)S(1)}, bf16[288,128]{1,0:T(8,128)(2,1)S(1)}, u32[]{:S(2)}, u32[]{:S(2)}) %collective-permute-start.34) | collective-permute-done | bytes 73760 | tf_op jit(solution)/shard_map/ppermute | solution.py:1038
  (67 shorter events, 15.4 us)
Async XLA Ops:
  1.3 14.1 %collective-permute-start.2 = (bf16[576,256]{1,0:T(8,128)(2,1)S(1)}, bf16[576,256]{1,0:T(8,128)(2,1)S(1)}, u32[]{:S(2)}, u32[]{:S(2)}) collective-permute-start(bf16[576,256]{1,0:T(8,128)(2,1)S(1)} %get-tuple-element.74.refs_2_), channel_id=1, source_target_pairs={{0,2},{2,0},{1,3},{3,1},{4,6},{6,4},{5,7},{7,5},{8,10},{10,8},{9,1... | collective-permute-start | bytes 884744 | tf_op jit(solution)/shard_map/ppermute | solution.py:773
  4.3 11.0 %collective-permute-start.1 = (bf16[576,128]{1,0:T(8,128)(2,1)}, bf16[576,128]{1,0:T(8,128)(2,1)S(1)}, u32[]{:S(2)}, u32[]{:S(2)}) collective-permute-start(bf16[576,128]{1,0:T(8,128)(2,1)} %bitcast.7), channel_id=1, source_target_pairs={{0,2},{2,0},{1,3},{3,1},{4,6},{6,4},{5,7},{7,5},{8,10},{10,8},{9,1... | collective-permute-start | bytes 442376 | tf_op jit(solution)/shard_map/ppermute | solution.py:773
  4.4 17.3 %collective-permute-start.3 = (bf16[576,256]{1,0:T(8,128)(2,1)S(1)}, bf16[576,256]{1,0:T(8,128)(2,1)S(1)}, u32[]{:S(2)}, u32[]{:S(2)}) collective-permute-start(bf16[576,256]{1,0:T(8,128)(2,1)S(1)} %get-tuple-element.78.refs_0_.refs_3_), channel_id=1, source_target_pairs={{0,2},{2,0},{1,3},{3,1},{4,6},{6,4},{5,7},{7,5},{8,10},{10,8},{9,1... | collective-permute-start | bytes 884744 | tf_op jit(solution)/shard_map/ppermute | solution.py:773
  6.3 21.6 %collective-permute-start = (bf16[576,256]{1,0:T(8,128)(2,1)S(1)}, bf16[576,256]{1,0:T(8,128)(2,1)S(1)}, u32[]{:S(2)}, u32[]{:S(2)}) collective-permute-start(bf16[576,256]{1,0:T(8,128)(2,1)S(1)} %get-tuple-element.73.refs_0_.refs_2_), channel_id=1, source_target_pairs={{0,2},{2,0},{1,3},{3,1},{4,6},{6,4},{5,7},{7,5},{8,10},{10,8},{9,1... | collective-permute-start | bytes 884744 | tf_op jit(solution)/shard_map/ppermute | solution.py:773
  6.4 27.0 %collective-permute-start.4 = (bf16[576,256]{1,0:T(8,128)(2,1)S(1)}, bf16[576,256]{1,0:T(8,128)(2,1)S(1)}, u32[]{:S(2)}, u32[]{:S(2)}) collective-permute-start(bf16[576,256]{1,0:T(8,128)(2,1)S(1)} %get-tuple-element.83.refs_0_.refs_3_), channel_id=1, source_target_pairs={{0,2},{2,0},{1,3},{3,1},{4,6},{6,4},{5,7},{7,5},{8,10},{10,8},{9,1... | collective-permute-start | bytes 884744 | tf_op jit(solution)/shard_map/ppermute | solution.py:773
  11.0 4.3 %copy-start.3 = (bf16[1,1,576,128]{3,2,1,0:T(8,128)(2,1)S(1)}, bf16[1,1,576,128]{3,2,1,0:T(8,128)(2,1)}, u32[]{:S(2)}) copy-start(bf16[1,1,576,128]{3,2,1,0:T(8,128)(2,1)} %param.12) | copy-start | bytes 442372
  37.1 32.8 %collective-permute-start.20 = (bf16[288,1152]{1,0:T(8,128)(2,1)S(1)}, bf16[288,1152]{1,0:T(8,128)(2,1)S(1)}, u32[]{:S(2)}, u32[]{:S(2)}) collective-permute-start(bf16[288,1152]{1,0:T(8,128)(2,1)S(1)} %get-tuple-element.116), channel_id=1, source_target_pairs={{0,2},{2,0},{1,3},{3,1},{4,6},{6,4},{5,7},{7,5},{8,10},{10,8},{9,1... | collective-permute-start | bytes 1990664 | tf_op jit(solution)/shard_map/ppermute | solution.py:773
  38.9 17.9 %collective-permute-start.6 = (bf16[72,1152]{1,0:T(8,128)(2,1)S(1)}, bf16[72,1152]{1,0:T(8,128)(2,1)S(1)}, u32[]{:S(2)}, u32[]{:S(2)}) collective-permute-start(bf16[72,1152]{1,0:T(8,128)(2,1)S(1)} %get-tuple-element.89), channel_id=1, source_target_pairs={{0,2},{2,0},{1,3},{3,1},{4,6},{6,4},{5,7},{7,5},{8,10},{10,8},{9,1... | collective-permute-start | bytes 497672 | tf_op jit(solution)/shard_map/ppermute | solution.py:773
  56.8 5.3 %collective-permute-start.7 = (bf16[72,1152]{1,0:T(8,128)(2,1)S(1)}, bf16[72,1152]{1,0:T(8,128)(2,1)S(1)}, u32[]{:S(2)}, u32[]{:S(2)}) collective-permute-start(bf16[72,1152]{1,0:T(8,128)(2,1)S(1)} %collective-permute-done.6.own), channel_id=1, source_target_pairs={{0,4},{4,0},{8,12},{12,8},{1,5},{5,1},{9,13},{13,9},{2,6},{6,2},{1... | collective-permute-start | bytes 497672 | tf_op jit(solution)/shard_map/ppermute | solution.py:887
  62.5 10.3 %collective-permute-start.10 = (bf16[144,1152]{1,0:T(8,128)(2,1)S(1)}, bf16[144,1152]{1,0:T(8,128)(2,1)S(1)}, u32[]{:S(2)}, u32[]{:S(2)}) collective-permute-start(bf16[144,1152]{1,0:T(8,128)(2,1)S(1)} %shard_map.121.refs_13_.refs_10_), channel_id=1, source_target_pairs={{0,16},{16,0},{1,17},{17,1},{2,18},{18,2},{3,19},{19,3},{4,20},{20... | collective-permute-start | bytes 995336 | tf_op jit(solution)/shard_map/ppermute | solution.py:773
  64.1 7.4 %collective-permute-start.8 = (bf16[576,256]{1,0:T(8,128)(2,1)S(1)}, bf16[576,256]{1,0:T(8,128)(2,1)S(1)}, u32[]{:S(2)}, u32[]{:S(2)}) collective-permute-start(bf16[576,256]{1,0:T(8,128)(2,1)S(1)} %shard_map.119), channel_id=1, source_target_pairs={{0,2},{2,0},{1,3},{3,1},{4,6},{6,4},{5,7},{7,5},{8,10},{10,8},{9,1... | collective-permute-start | bytes 884744 | tf_op jit(solution)/shard_map/ppermute | solution.py:773
  65.6 5.9 %copy-start.1 = (bf16[576,1152]{1,0:T(8,128)(2,1)S(1)}, bf16[576,1152]{1,0:T(8,128)(2,1)}, u32[]{:S(2)}) copy-start(bf16[576,1152]{1,0:T(8,128)(2,1)} %refs_12_.1) | copy-start | bytes 3981316
  65.6 9.2 %collective-permute-start.18 = (bf16[72,1152]{1,0:T(8,128)(2,1)S(1)}, bf16[72,1152]{1,0:T(8,128)(2,1)S(1)}, u32[]{:S(2)}, u32[]{:S(2)}) collective-permute-start(bf16[72,1152]{1,0:T(8,128)(2,1)S(1)} %get-tuple-element.112), channel_id=1, source_target_pairs={{0,2},{2,0},{1,3},{3,1},{4,6},{6,4},{5,7},{7,5},{8,10},{10,8},{9,1... | collective-permute-start | bytes 497672 | tf_op jit(solution)/shard_map/ppermute | solution.py:773
  69.9 31.2 %collective-permute-start.24 = (bf16[288,1152]{1,0:T(8,128)(2,1)S(1)}, bf16[288,1152]{1,0:T(8,128)(2,1)S(1)}, u32[]{:S(2)}, u32[]{:S(2)}) collective-permute-start(bf16[288,1152]{1,0:T(8,128)(2,1)S(1)} %collective-permute-done.20.refs_5_), channel_id=1, source_target_pairs={{0,16},{16,0},{1,17},{17,1},{2,18},{18,2},{3,19},{19,3},{4,20},{20... | collective-permute-start | bytes 1990664 | tf_op jit(solution)/shard_map/ppermute | solution.py:773
  72.7 9.0 %collective-permute-start.9 = (bf16[144,1152]{1,0:T(8,128)(2,1)S(1)}, bf16[144,1152]{1,0:T(8,128)(2,1)S(1)}, u32[]{:S(2)}, u32[]{:S(2)}) collective-permute-start(bf16[144,1152]{1,0:T(8,128)(2,1)S(1)} %shard_map.121.refs_13_.refs_10_), channel_id=1, source_target_pairs={{0,1},{1,0},{2,3},{3,2},{4,5},{5,4},{6,7},{7,6},{8,9},{9,8},{10,11... | collective-permute-start | bytes 995336 | tf_op jit(solution)/shard_map/ppermute | solution.py:773
  72.8 11.6 %collective-permute-start.11 = (bf16[144,1152]{1,0:T(8,128)(2,1)S(1)}, bf16[144,1152]{1,0:T(8,128)(2,1)S(1)}, u32[]{:S(2)}, u32[]{:S(2)}) collective-permute-start(bf16[144,1152]{1,0:T(8,128)(2,1)S(1)} %collective-permute-done.10.refs_15_.refs_12_), channel_id=1, source_target_pairs={{0,1},{1,0},{2,3},{3,2},{4,5},{5,4},{6,7},{7,6},{8,9},{9,8},{10,11... | collective-permute-start | bytes 995336 | tf_op jit(solution)/shard_map/ppermute | solution.py:773
  73.3 12.8 %collective-permute-start.5 = (bf16[576,256]{1,0:T(8,128)(2,1)S(1)}, bf16[576,256]{1,0:T(8,128)(2,1)S(1)}, u32[]{:S(2)}, u32[]{:S(2)}) collective-permute-start(bf16[576,256]{1,0:T(8,128)(2,1)S(1)} %shard_map.118), channel_id=1, source_target_pairs={{0,2},{2,0},{1,3},{3,1},{4,6},{6,4},{5,7},{7,5},{8,10},{10,8},{9,1... | collective-permute-start | bytes 884744 | tf_op jit(solution)/shard_map/ppermute | solution.py:773
  74.8 6.0 %collective-permute-start.19 = (bf16[72,1152]{1,0:T(8,128)(2,1)S(1)}, bf16[72,1152]{1,0:T(8,128)(2,1)S(1)}, u32[]{:S(2)}, u32[]{:S(2)}) collective-permute-start(bf16[72,1152]{1,0:T(8,128)(2,1)S(1)} %collective-permute-done.18.own), channel_id=1, source_target_pairs={{0,4},{4,0},{8,12},{12,8},{1,5},{5,1},{9,13},{13,9},{2,6},{6,2},{1... | collective-permute-start | bytes 497672 | tf_op jit(solution)/shard_map/ppermute | solution.py:887
  80.8 10.1 %collective-permute-start.27 = (bf16[144,1152]{1,0:T(8,128)(2,1)S(1)}, bf16[144,1152]{1,0:T(8,128)(2,1)S(1)}, u32[]{:S(2)}, u32[]{:S(2)}) collective-permute-start(bf16[144,1152]{1,0:T(8,128)(2,1)S(1)} %get-tuple-element.124), channel_id=1, source_target_pairs={{0,2},{2,0},{1,3},{3,1},{4,6},{6,4},{5,7},{7,5},{8,10},{10,8},{9,1... | collective-permute-start | bytes 995336 | tf_op jit(solution)/shard_map/ppermute | solution.py:773
  81.7 20.0 %collective-permute-start.14 = (bf16[592,128]{1,0:T(8,128)(2,1)S(1)}, bf16[592,128]{1,0:T(8,128)(2,1)S(1)}, u32[]{:S(2)}, u32[]{:S(2)}) collective-permute-start(bf16[592,128]{1,0:T(8,128)(2,1)S(1)} %get-tuple-element.95), channel_id=1, source_target_pairs={{0,8},{4,12},{8,0},{12,4},{1,9},{5,13},{9,1},{13,5},{2,10},{6,14},... | collective-permute-start | bytes 454664 | tf_op jit(solution)/shard_map/ppermute | solution.py:974
  84.4 17.5 %collective-permute-start.23 = (bf16[144,1152]{1,0:T(8,128)(2,1)S(1)}, bf16[144,1152]{1,0:T(8,128)(2,1)S(1)}, u32[]{:S(2)}, u32[]{:S(2)}) collective-permute-start(bf16[144,1152]{1,0:T(8,128)(2,1)S(1)} %shard_map.127.refs_4_), channel_id=1, source_target_pairs={{0,16},{16,0},{1,17},{17,1},{2,18},{18,2},{3,19},{19,3},{4,20},{20... | collective-permute-start | bytes 995336 | tf_op jit(solution)/shard_map/ppermute | solution.py:773
  86.1 15.0 %collective-permute-start.16 = (bf16[576,128]{1,0:T(8,128)(2,1)S(1)}, bf16[576,128]{1,0:T(8,128)(2,1)S(1)}, u32[]{:S(2)}, u32[]{:S(2)}) collective-permute-start(bf16[576,128]{1,0:T(8,128)(2,1)S(1)} %get-tuple-element.104), channel_id=1, source_target_pairs={{0,8},{4,12},{8,0},{12,4},{1,9},{5,13},{9,1},{13,5},{2,10},{6,14},... | collective-permute-start | bytes 442376 | tf_op jit(solution)/shard_map/ppermute | solution.py:974
  90.8 14.2 %collective-permute-start.15 = (bf16[592,128]{1,0:T(8,128)(2,1)S(1)}, bf16[592,128]{1,0:T(8,128)(2,1)S(1)}, u32[]{:S(2)}, u32[]{:S(2)}) collective-permute-start(bf16[592,128]{1,0:T(8,128)(2,1)S(1)} %get-tuple-element.103), channel_id=1, source_target_pairs={{0,12},{4,8},{8,4},{12,0},{1,13},{5,9},{9,5},{13,1},{2,14},{6,10},... | collective-permute-start | bytes 454664 | tf_op jit(solution)/shard_map/ppermute | solution.py:974
  94.2 26.5 %copy-start = (bf16[3,576,1152]{2,1,0:T(8,128)(2,1)S(1)}, bf16[3,576,1152]{2,1,0:T(8,128)(2,1)}, u32[]{:S(2)}) copy-start(bf16[3,576,1152]{2,1,0:T(8,128)(2,1)} %refs_5_.3) | copy-start | bytes 11943940
  101.1 24.7 %collective-permute-start.22 = (bf16[288,1152]{1,0:T(8,128)(2,1)S(1)}, bf16[288,1152]{1,0:T(8,128)(2,1)S(1)}, u32[]{:S(2)}, u32[]{:S(2)}) collective-permute-start(bf16[288,1152]{1,0:T(8,128)(2,1)S(1)} %collective-permute-done.20.refs_5_), channel_id=1, source_target_pairs={{0,1},{1,0},{2,3},{3,2},{4,5},{5,4},{6,7},{7,6},{8,9},{9,8},{10,11... | collective-permute-start | bytes 1990664 | tf_op jit(solution)/shard_map/ppermute | solution.py:773
  101.1 15.5 %collective-permute-start.29 = (bf16[144,1152]{1,0:T(8,128)(2,1)S(1)}, bf16[144,1152]{1,0:T(8,128)(2,1)S(1)}, u32[]{:S(2)}, u32[]{:S(2)}) collective-permute-start(bf16[144,1152]{1,0:T(8,128)(2,1)S(1)} %collective-permute-done.27.refs_7_), channel_id=1, source_target_pairs={{0,16},{16,0},{1,17},{17,1},{2,18},{18,2},{3,19},{19,3},{4,20},{20... | collective-permute-start | bytes 995336 | tf_op jit(solution)/shard_map/ppermute | solution.py:773
  101.7 24.1 %collective-permute-start.26 = (bf16[288,1152]{1,0:T(8,128)(2,1)S(1)}, bf16[288,1152]{1,0:T(8,128)(2,1)S(1)}, u32[]{:S(2)}, u32[]{:S(2)}) collective-permute-start(bf16[288,1152]{1,0:T(8,128)(2,1)S(1)} %collective-permute-done.24.refs_9_), channel_id=1, source_target_pairs={{0,1},{1,0},{2,3},{3,2},{4,5},{5,4},{6,7},{7,6},{8,9},{9,8},{10,11... | collective-permute-start | bytes 1990664 | tf_op jit(solution)/shard_map/ppermute | solution.py:773
  101.9 7.9 %collective-permute-start.17 = (bf16[576,128]{1,0:T(8,128)(2,1)S(1)}, bf16[576,128]{1,0:T(8,128)(2,1)S(1)}, u32[]{:S(2)}, u32[]{:S(2)}) collective-permute-start(bf16[576,128]{1,0:T(8,128)(2,1)S(1)} %get-tuple-element.105), channel_id=1, source_target_pairs={{0,12},{4,8},{8,4},{12,0},{1,13},{5,9},{9,5},{13,1},{2,14},{6,10},... | collective-permute-start | bytes 442376 | tf_op jit(solution)/shard_map/ppermute | solution.py:974
  105.1 15.1 %collective-permute-start.25 = (bf16[144,1152]{1,0:T(8,128)(2,1)S(1)}, bf16[144,1152]{1,0:T(8,128)(2,1)S(1)}, u32[]{:S(2)}, u32[]{:S(2)}) collective-permute-start(bf16[144,1152]{1,0:T(8,128)(2,1)S(1)} %collective-permute-done.23.refs_8_), channel_id=1, source_target_pairs={{0,1},{1,0},{2,3},{3,2},{4,5},{5,4},{6,7},{7,6},{8,9},{9,8},{10,11... | collective-permute-start | bytes 995336 | tf_op jit(solution)/shard_map/ppermute | solution.py:773
  109.9 5.1 %collective-permute-start.13 = (bf16[576,128]{1,0:T(8,128)(2,1)S(1)}, bf16[576,128]{1,0:T(8,128)(2,1)S(1)}, u32[]{:S(2)}, u32[]{:S(2)}) collective-permute-start(bf16[576,128]{1,0:T(8,128)(2,1)S(1)} %get-tuple-element.102), channel_id=1, source_target_pairs={{0,4},{4,0},{8,12},{12,8},{1,5},{5,1},{9,13},{13,9},{2,6},{6,2},{1... | collective-permute-start | bytes 442376 | tf_op jit(solution)/shard_map/ppermute | solution.py:974
  115.0 5.2 %collective-permute-start.12 = (bf16[592,128]{1,0:T(8,128)(2,1)S(1)}, bf16[592,128]{1,0:T(8,128)(2,1)S(1)}, u32[]{:S(2)}, u32[]{:S(2)}) collective-permute-start(bf16[592,128]{1,0:T(8,128)(2,1)S(1)} %get-tuple-element.100), channel_id=1, source_target_pairs={{0,4},{4,0},{8,12},{12,8},{1,5},{5,1},{9,13},{13,9},{2,6},{6,2},{1... | collective-permute-start | bytes 454664 | tf_op jit(solution)/shard_map/ppermute | solution.py:974
  116.6 9.1 %collective-permute-start.21 = (bf16[144,1152]{1,0:T(8,128)(2,1)S(1)}, bf16[144,1152]{1,0:T(8,128)(2,1)S(1)}, u32[]{:S(2)}, u32[]{:S(2)}) collective-permute-start(bf16[144,1152]{1,0:T(8,128)(2,1)S(1)} %shard_map.127.refs_4_), channel_id=1, source_target_pairs={{0,1},{1,0},{2,3},{3,2},{4,5},{5,4},{6,7},{7,6},{8,9},{9,8},{10,11... | collective-permute-start | bytes 995336 | tf_op jit(solution)/shard_map/ppermute | solution.py:773
  120.2 9.2 %collective-permute-start.28 = (bf16[144,1152]{1,0:T(8,128)(2,1)S(1)}, bf16[144,1152]{1,0:T(8,128)(2,1)S(1)}, u32[]{:S(2)}, u32[]{:S(2)}) collective-permute-start(bf16[144,1152]{1,0:T(8,128)(2,1)S(1)} %collective-permute-done.27.refs_7_), channel_id=1, source_target_pairs={{0,1},{1,0},{2,3},{3,2},{4,5},{5,4},{6,7},{7,6},{8,9},{9,8},{10,11... | collective-permute-start | bytes 995336 | tf_op jit(solution)/shard_map/ppermute | solution.py:773
  120.2 9.2 %collective-permute-start.30 = (bf16[144,1152]{1,0:T(8,128)(2,1)S(1)}, bf16[144,1152]{1,0:T(8,128)(2,1)S(1)}, u32[]{:S(2)}, u32[]{:S(2)}) collective-permute-start(bf16[144,1152]{1,0:T(8,128)(2,1)S(1)} %collective-permute-done.29.refs_9_), channel_id=1, source_target_pairs={{0,1},{1,0},{2,3},{3,2},{4,5},{5,4},{6,7},{7,6},{8,9},{9,8},{10,11... | collective-permute-start | bytes 995336 | tf_op jit(solution)/shard_map/ppermute | solution.py:773
  125.8 3.6 %copy-start.2 = (bf16[576,1152]{1,0:T(8,128)(2,1)S(1)}, bf16[576,1152]{1,0:T(8,128)(2,1)}, u32[]{:S(2)}) copy-start(bf16[576,1152]{1,0:T(8,128)(2,1)} %refs_6_.3) | copy-start | bytes 3981316
  131.0 2.2 %collective-permute-start.35 = (bf16[2,2,288,128]{3,2,1,0:T(8,128)(2,1)S(1)}, bf16[2,2,288,128]{3,2,1,0:T(8,128)(2,1)S(1)}, u32[]{:S(2)}, u32[]{:S(2)}) collective-permute-start(bf16[2,2,288,128]{3,2,1,0:T(8,128)(2,1)S(1)} %get-tuple-element.135), channel_id=1, source_target_pairs={{0,1},{1,0},{2,3},{3,2},{4,5},{5,4},{6,7},{7,6},{8,9},{9,8},{10,11... | collective-permute-start | bytes 884744 | tf_op jit(solution)/shard_map/ppermute | solution.py:773
  132.7 9.0 %collective-permute-start.31 = (bf16[2,2,288,128]{3,2,1,0:T(8,128)(2,1)S(1)}, bf16[2,2,288,128]{3,2,1,0:T(8,128)(2,1)S(1)}, u32[]{:S(2)}, u32[]{:S(2)}) collective-permute-start(bf16[2,2,288,128]{3,2,1,0:T(8,128)(2,1)S(1)} %get-tuple-element.128), channel_id=1, source_target_pairs={{0,1},{1,0},{2,3},{3,2},{4,5},{5,4},{6,7},{7,6},{8,9},{9,8},{10,11... | collective-permute-start | bytes 884744 | tf_op jit(solution)/shard_map/ppermute | solution.py:773
  133.9 10.0 %collective-permute-start.36 = (bf16[288,128]{1,0:T(8,128)(2,1)S(1)}, bf16[288,128]{1,0:T(8,128)(2,1)S(1)}, u32[]{:S(2)}, u32[]{:S(2)}) collective-permute-start(bf16[288,128]{1,0:T(8,128)(2,1)S(1)} %get-tuple-element.137), channel_id=1, source_target_pairs={{0,8},{2,10},{4,12},{6,14},{8,0},{10,2},{12,4},{14,6},{1,9},{3,11}... | collective-permute-start | bytes 221192 | tf_op jit(solution)/shard_map/ppermute | solution.py:1038
  136.3 12.3 %collective-permute-start.37 = (bf16[288,128]{1,0:T(8,128)(2,1)S(1)}, bf16[288,128]{1,0:T(8,128)(2,1)S(1)}, u32[]{:S(2)}, u32[]{:S(2)}) collective-permute-start(bf16[288,128]{1,0:T(8,128)(2,1)S(1)} %get-tuple-element.138), channel_id=1, source_target_pairs={{0,10},{2,8},{4,14},{6,12},{8,2},{10,0},{12,6},{14,4},{1,11},{3,9}... | collective-permute-start | bytes 221192 | tf_op jit(solution)/shard_map/ppermute | solution.py:1038
  137.9 10.8 %collective-permute-start.38 = (bf16[288,128]{1,0:T(8,128)(2,1)S(1)}, bf16[288,128]{1,0:T(8,128)(2,1)S(1)}, u32[]{:S(2)}, u32[]{:S(2)}) collective-permute-start(bf16[288,128]{1,0:T(8,128)(2,1)S(1)} %get-tuple-element.139), channel_id=1, source_target_pairs={{0,12},{2,14},{4,8},{6,10},{8,4},{10,6},{12,0},{14,2},{1,13},{3,15... | collective-permute-start | bytes 221192 | tf_op jit(solution)/shard_map/ppermute | solution.py:1038
  141.0 7.6 %collective-permute-start.39 = (bf16[288,128]{1,0:T(8,128)(2,1)S(1)}, bf16[288,128]{1,0:T(8,128)(2,1)S(1)}, u32[]{:S(2)}, u32[]{:S(2)}) collective-permute-start(bf16[288,128]{1,0:T(8,128)(2,1)S(1)} %get-tuple-element.140), channel_id=1, source_target_pairs={{0,14},{2,12},{4,10},{6,8},{8,6},{10,4},{12,2},{14,0},{1,15},{3,13... | collective-permute-start | bytes 221192 | tf_op jit(solution)/shard_map/ppermute | solution.py:1038
  142.4 6.5 %collective-permute-start.32 = (bf16[288,128]{1,0:T(8,128)(2,1)S(1)}, bf16[288,128]{1,0:T(8,128)(2,1)S(1)}, u32[]{:S(2)}, u32[]{:S(2)}) collective-permute-start(bf16[288,128]{1,0:T(8,128)(2,1)S(1)} %get-tuple-element.131), channel_id=1, source_target_pairs={{0,2},{2,0},{4,6},{6,4},{8,10},{10,8},{12,14},{14,12},{1,3},{3,1},... | collective-permute-start | bytes 221192 | tf_op jit(solution)/shard_map/ppermute | solution.py:1038
  144.0 5.0 %collective-permute-start.33 = (bf16[288,128]{1,0:T(8,128)(2,1)S(1)}, bf16[288,128]{1,0:T(8,128)(2,1)S(1)}, u32[]{:S(2)}, u32[]{:S(2)}) collective-permute-start(bf16[288,128]{1,0:T(8,128)(2,1)S(1)} %get-tuple-element.132), channel_id=1, source_target_pairs={{0,4},{2,6},{4,0},{6,2},{8,12},{10,14},{12,8},{14,10},{1,5},{3,7},... | collective-permute-start | bytes 221192 | tf_op jit(solution)/shard_map/ppermute | solution.py:1038
  148.7 5.3 %collective-permute-start.34 = (bf16[288,128]{1,0:T(8,128)(2,1)S(1)}, bf16[288,128]{1,0:T(8,128)(2,1)S(1)}, u32[]{:S(2)}, u32[]{:S(2)}) collective-permute-start(bf16[288,128]{1,0:T(8,128)(2,1)S(1)} %get-tuple-element.133), channel_id=1, source_target_pairs={{0,6},{2,4},{4,2},{6,0},{8,14},{10,12},{12,10},{14,8},{1,7},{3,5},... | collective-permute-start | bytes 221192 | tf_op jit(solution)/shard_map/ppermute | solution.py:1038
where the time goes:
time: 155 us
  waiting for transfers between devices  57.2 us (37%)
  Pallas kernels  49.3 us (32%)
  starting transfers between devices  45.2 us (29%)
  between operations  2.45 us (2%)
    pallas_call x20, Pallas kernels, resident(): pl.pallas_call(kernel, out_shape=tuple((kind(shape, dtype) for shape, dty...  43.4 us
    ppermute x25, waiting for transfers between devices, shift(): return lax.ppermute(x, axis, [(i, (i + by) % size) for i in range(size)])  24.8 us
    ppermute x25, starting transfers between devices, shift(): return lax.ppermute(x, axis, [(i, (i + by) % size) for i in range(size)])  18.4 us
    ppermute x6, waiting for transfers between devices, send_all(): x = lax.ppermute(x, SEQ, route)  17.1 us
    ppermute x6, starting transfers between devices, send_all(): x = lax.ppermute(x, SEQ, route)  13.1 us
    ppermute x7, starting transfers between devices, shards_fast(): piece = lax.ppermute(piece, (SEQ, HEADS), route)  10.6 us
    ppermute x7, waiting for transfers between devices, shards_fast(): piece = lax.ppermute(piece, (SEQ, HEADS), route)  8.66 us
    ppermute x2, waiting for transfers between devices, trade(): held[r, 0, 0] = (own, lax.ppermute(own, SEQ, pairs))  6.64 us
  transfers between devices with their start and end apart: 40, of which 15 were waited for; matrix products, arithmetic and copies ran while one was open for 1% of the time, Pallas kernels for 27%

commit v1 on v0

--- a/solution.py
+++ b/solution.py
@@ -573,69 +573,72 @@
     )[0]
 
 
-def time_out_kernel(frames, parts, share, keys, first, info, *refs):
+def time_out_kernel(frames, parts, share, keys, first, own, info, *refs):
     near, refs = refs[:frames], refs[frames:]
     far, refs = refs[:frames], refs[frames:]
-    att_near, att_far, o_own, refs = refs[0], refs[1], refs[2], refs[3:]
+    att_near, att_far, refs = refs[0], refs[1], refs[2:]
+    o_own, refs = (refs[0], refs[1:]) if own else (None, refs)
     o_far, (keep, send, ratios, att, res) = refs[: len(keys)], refs[len(keys) :]
     lanes = near[0].shape[1]
-    width = o_own.shape[0]
+    width = att_near.shape[0]
     head_index, branch = place_of(HEADS), place_of(CFG)
+    cols = slice(first * lanes, (first + frames) * lanes)
     for r in range(parts):
         span = pl.ds(aligned(base_of(parts, r, width)), width)
-        cols = slice(first * lanes, (first + frames) * lanes)
         att[span, :] = (
             att_near[:, cols] if r == 0 else att_far[(r - 1) * width : r * width, cols]
         )
-    far_y = jnp.dot(
-        jnp.concatenate([x[...] for x in o_far], axis=0),
-        att[...],
-        preferred_element_type=jnp.float32,
-    )
+
+    def add(y, source, start, rows):
+        for f in range(frames):
+            x = source[f][start, :].astype(jnp.float32) + y[:, f * lanes : (f + 1) * lanes]
+            res[f, rows, :] = x.astype(jnp.bfloat16)
+
+    if own:
+        y = jnp.dot(o_own[...], att[...], preferred_element_type=jnp.float32)
+        add(y, near, slice(0, width), pl.ds(aligned(base_of(parts, 0, width)), width))
+    if keys:
+        far_y = jnp.dot(
+            jnp.concatenate([x[...] for x in o_far], axis=0),
+            att[...],
+            preferred_element_type=jnp.float32,
+        )
     done = 0
-    for key in [(0, 0, 0)] + list(keys):
-        base = base_of(parts, key[0], width)
-        if key[0]:
-            count = o_far[keys.index(key)].shape[0]
-            offset = quarter_of(key, count, *share)
-            source, start = far, (key[0] - 1) * width + offset
-            y = far_y[done : done + count]
-            done += count
-        else:
-            count, offset, source, start = width, 0, near, 0
-            y = jnp.dot(o_own[...], att[...], preferred_element_type=jnp.float32)
-        for f in range(frames):
-            if key[0]:
-                x = source[f][pl.ds(aligned(start), count), :]
-            else:
-                x = source[f][0:count, :]
-            x = x.astype(jnp.float32) + y[:, f * lanes : (f + 1) * lanes]
-            res[f, pl.ds(aligned(base + offset), count), :] = x.astype(jnp.bfloat16)
+    for i, key in enumerate(keys):
+        count = o_far[i].shape[0]
+        offset = quarter_of(key, count, *share)
+        add(
+            far_y[done : done + count],
+            far,
+            pl.ds(aligned((key[0] - 1) * width + offset), count),
+            pl.ds(aligned(base_of(parts, key[0], width) + offset), count),
+        )
+        done += count
     slot = keep.shape[2]
     for f in range(frames):
         tail = near[f][width:, :].astype(jnp.float32)
         ratios[f : f + 1, :] = tail[0:1] / tail[1:2]
-        for r in range(parts):
-            head = lax.rem(head_index + r, parts)
-            keep[f, r] = res[f, pl.ds(aligned((head * 2 + branch) * slot), slot), :]
-            send[f, r] = res[f, pl.ds(aligned((head * 2 + 1 - branch) * slot), slot), :]
-
-
-def time_out_call(
-    info, near, far, att_near, att_far, o_own, o_far, parts, share, keys, first
-):
+        for n in range(keep.shape[1]):
+            head = lax.rem(head_index + n + (0 if own else 1), parts)
+            keep[f, n] = res[f, pl.ds(aligned((head * 2 + branch) * slot), slot), :]
+            send[f, n] = res[f, pl.ds(aligned((head * 2 + 1 - branch) * slot), slot), :]
+
+
+def time_out_call(info, near, far, att_near, att_far, o_own, o_far, parts, share, keys, first):
     frames, lanes = len(near), near[0].shape[1]
-    result = ((frames, parts, D // (2 * parts), lanes), jnp.bfloat16)
+    own = [] if o_own is None else [o_own]
+    count = len(own) + (parts - 1 if keys else 0)
+    result = ((frames, count, D // (2 * parts), lanes), jnp.bfloat16)
     return resident(
-        functools.partial(time_out_kernel, frames, parts, share, keys, first),
+        functools.partial(time_out_kernel, frames, parts, share, keys, first, bool(own)),
         [result, result, ((frames, lanes), jnp.float32)],
         info,
-        list(near) + list(far) + [att_near, att_far, o_own] + list(o_far),
+        list(near) + list(far) + [att_near, att_far] + own + list(o_far),
         [
             pltpu.VMEM((D, frames * lanes), jnp.bfloat16),
             pltpu.VMEM((frames, D, lanes), jnp.bfloat16),
         ],
-        2 * D * D * frames * lanes,
+        2 * D * D * frames * lanes * count // parts,
         12,
     )
 
@@ -961,7 +964,7 @@
     late = out_rows(0, 1, 1)
     far_time.append(first_hop(mine[2], first))
     far_last = first_hop(mine[3], second)
-    for held, gate in zip(far_time, (early, second)):
+    for name, held, gate in zip("qk", far_time, (early, middle)):
         second_hop(held, gate)
         third_hop(held, late)
 
@@ -998,37 +1001,42 @@
     slot = D // (heads * cfg)
     landed = {}
     results = {}
-    for cross in (1, 0):
+    jobs = [(1, 1, 0), (1, 0, 1), (0, 1, 1)]
+    for cross, own, others in jobs:
+        name = f"{cross}{own}"
         picked = [i for i, road in enumerate(roads(seq)) if road[0] == cross]
+        part = keys * others
         keep, send, ratios = time_out_call(
             info,
             [near[i] for i in picked],
             [far[i] for i in picked],
             att_near,
             att_far,
-            temporal_out,
-            [far_last[key] for key in keys],
+            temporal_out if own else None,
+            [far_last[key] for key in part],
             heads,
             split,
-            keys,
+            part,
             picked[0],
         )
-        results[cross] = keep, shift(send, CFG, 1), ratios
-    for cross in (1, 0):
+        results[name] = keep, shift(send, CFG, 1), ratios
+    for cross, own, others in jobs:
+        name = f"{cross}{own}"
         picked = [i for i, road in enumerate(roads(seq)) if road[0] == cross]
+        sides = list(range(1 - own, 1 + (heads - 1) * others))
         pieces = resident(
             guide_kernel,
-            [((slot, lanes), jnp.bfloat16)] * (len(picked) * heads),
+            [((slot, lanes), jnp.bfloat16)] * (len(picked) * len(sides)),
             info,
-            results[cross],
+            results[name],
             [],
             len(picked) * D * lanes,
             8,
         )
         for n, i in enumerate(picked):
             road = roads(seq)[i]
-            for r in range(heads):
-                piece = pieces[n * heads + r]
+            for k, r in enumerate(sides):
+                piece = pieces[n * len(sides) + k]
                 if road != (0, 0) or r:
                     route = [
                         (a * heads + b, follow(seq, road, a, True) * heads + (b + r) % heads)

time: 155 us -> 149 us (0.961)
  waiting for transfers between devices: 57.2 us -> 48.5 us
    ppermute x25 -> x26, waiting for transfers between devices: 24.8 us -> 19.8 us  [shift(): return lax.ppermute(x, axis, [(i, (i + by) % size) for i in range(size)])]
    ppermute x25 -> x26, starting transfers between devices: 18.4 us -> 21 us  [shift(): return lax.ppermute(x, axis, [(i, (i + by) % size) for i in range(size)])]
    ppermute x6, starting transfers between devices: 13.1 us -> 11.3 us  [send_all(): x = lax.ppermute(x, SEQ, route)]
    ppermute x7, waiting for transfers between devices: 8.66 us -> 6.93 us  [shards_fast(): piece = lax.ppermute(piece, (SEQ, HEADS), route)]
    ppermute x6, waiting for transfers between devices: 17.1 us -> 15.5 us  [send_all(): x = lax.ppermute(x, SEQ, route)]
    pallas_call x20 -> x22, Pallas kernels: 43.4 us -> 44.8 us  [resident(): pl.pallas_call(kernel, out_shape=tuple((kind(shape, dtype) for shape, dty...]
  transfers between devices with their start and end apart: 40 -> 41, of which waited for: 15 -> 16; matrix products, arithmetic and copies ran while one was open for 1% -> 1% of each run, Pallas kernels for 27% -> 31%
where the time goes in v1:
time: 149 us
  Pallas kernels  50.7 us (34%)
  waiting for transfers between devices  48.5 us (33%)
  starting transfers between devices  46.1 us (31%)
  between operations  2.47 us (2%)
    pallas_call x22, Pallas kernels, resident(): pl.pallas_call(kernel, out_shape=tuple((kind(shape, dtype) for shape, dty...  44.8 us
    ppermute x26, starting transfers between devices, shift(): return lax.ppermute(x, axis, [(i, (i + by) % size) for i in range(size)])  21 us
    ppermute x26, waiting for transfers between devices, shift(): return lax.ppermute(x, axis, [(i, (i + by) % size) for i in range(size)])  19.8 us
    ppermute x6, waiting for transfers between devices, send_all(): x = lax.ppermute(x, SEQ, route)  15.5 us
    ppermute x6, starting transfers between devices, send_all(): x = lax.ppermute(x, SEQ, route)  11.3 us
    ppermute x7, starting transfers between devices, shards_fast(): piece = lax.ppermute(piece, (SEQ, HEADS), route)  10.1 us
    ppermute x7, waiting for transfers between devices, shards_fast(): piece = lax.ppermute(piece, (SEQ, HEADS), route)  6.93 us
    ppermute x2, waiting for transfers between devices, trade(): held[r, 0, 0] = (own, lax.ppermute(own, SEQ, pairs))  6.25 us
  transfers between devices with their start and end apart: 41, of which 16 were waited for; matrix products, arithmetic and copies ran while one was open for 1% of the time, Pallas kernels for 31%

profile of v1, /device:TPU:0, one launch (start us, length us, event | category | flops | bytes accessed | tf_op | source)
XLA Modules:
  0.0 148.5 jit_solution(12148339575338080776)
XLA Ops:
  0.0 1.3 shard_map.109
  1.3 3.0 %collective-permute-start.2 = (bf16[576,256]{1,0:T(8,128)(2,1)S(1)}, bf16[576,256]{1,0:T(8,128)(2,1)S(1)}, u32[]{:S(2)}, u32[]{:S(2)}) collective-permute-start(bf16[576,256]{1,0:T(8,128)(2,1)S(1)} %get-tuple-element.77.refs_2_), channel_id=1, source_target_pairs={{0,2},{2,0},{1,3},{3,1},{4,6},{6,4},{5,7},{7,5},{8,10},{10,8},{9,1... | collective-permute-start | bytes 884744 | tf_op jit(solution)/shard_map/ppermute | solution.py:776
  4.4 1.9 %collective-permute-start.3 = (bf16[576,256]{1,0:T(8,128)(2,1)S(1)}, bf16[576,256]{1,0:T(8,128)(2,1)S(1)}, u32[]{:S(2)}, u32[]{:S(2)}) collective-permute-start(bf16[576,256]{1,0:T(8,128)(2,1)S(1)} %get-tuple-element.81.refs_0_.refs_3_), channel_id=1, source_target_pairs={{0,2},{2,0},{1,3},{3,1},{4,6},{6,4},{5,7},{7,5},{8,10},{10,8},{9,1... | collective-permute-start | bytes 884744 | tf_op jit(solution)/shard_map/ppermute | solution.py:776
  6.4 1.9 %collective-permute-start.4 = (bf16[576,256]{1,0:T(8,128)(2,1)S(1)}, bf16[576,256]{1,0:T(8,128)(2,1)S(1)}, u32[]{:S(2)}, u32[]{:S(2)}) collective-permute-start(bf16[576,256]{1,0:T(8,128)(2,1)S(1)} %get-tuple-element.86.refs_0_.refs_3_), channel_id=1, source_target_pairs={{0,2},{2,0},{1,3},{3,1},{4,6},{6,4},{5,7},{7,5},{8,10},{10,8},{9,1... | collective-permute-start | bytes 884744 | tf_op jit(solution)/shard_map/ppermute | solution.py:776
  11.0 2.9 %shard_map.110 = (bf16[72,1152]{1,0:T(8,128)(2,1)S(1)}, bf16[72,1152]{1,0:T(8,128)(2,1)S(1)}, bf16[288,1152]{1,0:T(8,128)(2,1)S(1)}, bf16[144,1152]{1,0:T(8,128)...) custom-call(bf16[576,1152]{1,0:T(8,128)(2,1)} %refs_12_.1, bf16[3,576,1152]{2,1,0:T(8,128)(2,1)} %refs_5_.3, ...), custom_call_target="tpu_custom_call" | custom-call | tf_op jit(solution)/shard_map/pallas_call | solution.py:837
  14.0 1.3 collective-permute-done.1.refs_1_
  15.3 2.0 %collective-permute-start.6 = (bf16[72,1152]{1,0:T(8,128)(2,1)S(1)}, bf16[72,1152]{1,0:T(8,128)(2,1)S(1)}, u32[]{:S(2)}, u32[]{:S(2)}) collective-permute-start(bf16[72,1152]{1,0:T(8,128)(2,1)S(1)} %get-tuple-element.92), channel_id=1, source_target_pairs={{0,2},{2,0},{1,3},{3,1},{4,6},{6,4},{5,7},{7,5},{8,10},{10,8},{9,1... | collective-permute-start | bytes 497672 | tf_op jit(solution)/shard_map/ppermute | solution.py:776
  17.4 2.8 %shard_map.111 = (bf16[2,8,80,128]{3,2,1,0:T(8,128)(2,1)S(1)}, bf16[3,8,80,256]{3,2,1,0:T(8,128)(2,1)S(1)}) custom-call(s32[3]{0:T(128)S(1)} %pad_add_fusion.info, bf16[576,128]{1,0:T(8,128)(2,1)S(1)} %bitcast.8, bf16[576,128]{1,0:T(8,128)(2,1)S(1)} %collective-permute-done.1.refs_1_, bf16[576,256]{1,0:T(8,128)(2,1)S(1)} %get-tuple-element.77.refs_2_, ...), custom_call_target="tpu_custom_call" | custom-call | flops 1528823808 | bytes 4875264 | tf_op jit(solution)/shard_map/pallas_call | solution.py:161
  20.2 1.5 collective-permute-done.3.refs_1_.refs_3_.refs_5_.refs_7_.refs_9_
  21.7 2.1 %shard_map.112.refs_1_.refs_3_ = bf16[3,8,80,256]{3,2,1,0:T(8,128)(2,1)S(1)} custom-call(s32[3]{0:T(128)S(1)} %pad_add_fusion.info, bf16[576,256]{1,0:T(8,128)(2,1)S(1)} %get-tuple-element.81.refs_0_.refs_3_, bf16[576,256]{1,0:T(8,128)(2,1)S(1)} %collective-permute-done.3.refs_1_.refs_3_.refs_5_.refs_7_.refs_9_, ...), custom_call_target="tpu_custom_call" | custom-call | flops 1019215872 | bytes 4580352 | tf_op jit(solution)/shard_map/pallas_call | solution.py:161
  23.8 4.1 %shard_map.113 = (f32[8,80,256]{2,1,0:T(8,128)S(1)}, f32[8,8,256]{2,1,0:T(8,128)S(1)}, f32[8,80,256]{2,1,0:T(8,128)S(1)}, f32[8,8,256]{2,1,0:T(8,128)S(1)}) custom-call(s32[3]{0:T(128)S(1)} %pad_add_fusion.info, bf16[3,8,80,256]{3,2,1,0:T(8,128)(2,1)S(1)} %get-tuple-element.80.refs_0_.refs_2_, bf16[3,8,80,256]{3,2,1,0:T(8,128)(2,1)S(1)} %shard_map.112.refs_1_.refs_3_, ...), custom_call_target="tpu_custom_call" | custom-call | flops 2684354560 | bytes 4259840 | tf_op jit(solution)/shard_map/pallas_call | solution.py:161
  28.0 2.1 %shard_map.114.refs_2_.refs_0_.refs_4_ = bf16[3,8,80,256]{3,2,1,0:T(8,128)(2,1)S(1)} custom-call(s32[3]{0:T(128)S(1)} %pad_add_fusion.info, bf16[576,256]{1,0:T(8,128)(2,1)S(1)} %get-tuple-element.76.refs_0_.refs_2_, bf16[576,256]{1,0:T(8,128)(2,1)S(1)} %collective-permute-done.refs_1_.refs_4_.refs_6_.refs_8_.refs_10_, ...), custom_call_target="tpu_custom_call" | custom-call | flops 1019215872 | bytes 4580352 | tf_op jit(solution)/shard_map/pallas_call | solution.py:161
  30.1 2.0 %shard_map.115 = (f32[8,80,256]{2,1,0:T(8,128)S(1)}, f32[8,8,256]{2,1,0:T(8,128)S(1)}, f32[8,80,256]{2,1,0:T(8,128)S(1)}, f32[8,8,256]{2,1,0:T(8,128)S(1)}) custom-call(s32[3]{0:T(128)S(1)} %pad_add_fusion.info, bf16[3,8,80,256]{3,2,1,0:T(8,128)(2,1)S(1)} %get-tuple-element.80.refs_0_.refs_2_, bf16[3,8,80,256]{3,2,1,0:T(8,128)(2,1)S(1)} %shard_map.112.refs_1_.refs_3_, ...), custom_call_target="tpu_custom_call" | custom-call | flops 1073741824 | bytes 4390912 | tf_op jit(solution)/shard_map/pallas_call | solution.py:161
  32.1 2.2 %collective-permute-done.4.refs_1_.refs_5_.refs_7_.refs_9_.refs_11_ = bf16[576,256]{1,0:T(8,128)(2,1)S(1)} collective-permute-done((bf16[576,256]{1,0:T(8,128)(2,1)S(1)}, bf16[576,256]{1,0:T(8,128)(2,1)S(1)}, u32[]{:S(2)}, u32[]{:S(2)}) %collective-permute-start.4) | collective-permute-done | bytes 294944 | tf_op jit(solution)/shard_map/ppermute | solution.py:776
  34.3 2.1 %shard_map.116.refs_1_.refs_5_.refs_2_ = bf16[3,8,80,256]{3,2,1,0:T(8,128)(2,1)S(1)} custom-call(s32[3]{0:T(128)S(1)} %pad_add_fusion.info, bf16[576,256]{1,0:T(8,128)(2,1)S(1)} %get-tuple-element.86.refs_0_.refs_3_, bf16[576,256]{1,0:T(8,128)(2,1)S(1)} %collective-permute-done.4.refs_1_.refs_5_.refs_7_.refs_9_.refs_11_, ...), custom_call_target="tpu_custom_call" | custom-call | flops 1019215872 | bytes 4580352 | tf_op jit(solution)/shard_map/pallas_call | solution.py:161
  36.4 1.5 %shard_map.119 = bf16[576,256]{1,0:T(8,128)(2,1)S(1)} custom-call(s32[3]{0:T(128)S(1)} %pad_add_fusion.info, bf16[3,8,80,256]{3,2,1,0:T(8,128)(2,1)S(1)} %get-tuple-element.80.refs_0_.refs_2_, bf16[3,8,80,256]{3,2,1,0:T(8,128)(2,1)S(1)} %shard_map.112.refs_1_.refs_3_, bf16[3,8,80,256]{3,2,1,0:T(8,128)(2,1)S(1)} %shard_map.116.refs_1_.refs_5_.refs_2_, ...), custom_call_target="tpu_custom_call" | custom-call | flops 536870912 | bytes 3670016 | tf_op jit(solution)/shard_map/pallas_call | solution.py:161
  38.0 2.2 %collective-permute-start.7 = (bf16[72,1152]{1,0:T(8,128)(2,1)S(1)}, bf16[72,1152]{1,0:T(8,128)(2,1)S(1)}, u32[]{:S(2)}, u32[]{:S(2)}) collective-permute-start(bf16[72,1152]{1,0:T(8,128)(2,1)S(1)} %collective-permute-done.6.own), channel_id=1, source_target_pairs={{0,4},{4,0},{8,12},{12,8},{1,5},{5,1},{9,13},{13,9},{2,6},{6,2},{1... | collective-permute-start | bytes 497672 | tf_op jit(solution)/shard_map/ppermute | solution.py:890
  40.1 1.5 %shard_map.120.refs_0_ = bf16[576,256]{1,0:T(8,128)(2,1)S(1)} custom-call(s32[3]{0:T(128)S(1)} %pad_add_fusion.info, bf16[3,8,80,256]{3,2,1,0:T(8,128)(2,1)S(1)} %get-tuple-element.80.refs_0_.refs_2_, bf16[3,8,80,256]{3,2,1,0:T(8,128)(2,1)S(1)} %shard_map.112.refs_1_.refs_3_, bf16[3,8,80,256]{3,2,1,0:T(8,128)(2,1)S(1)} %shard_map.116.refs_1_.refs_5_.refs_2_, ...), custom_call_target="tpu_custom_call" | custom-call | flops 536870912 | bytes 3670016 | tf_op jit(solution)/shard_map/pallas_call | solution.py:161
  41.7 1.8 %collective-permute-done.7.other = bf16[72,1152]{1,0:T(8,128)(2,1)S(1)} collective-permute-done((bf16[72,1152]{1,0:T(8,128)(2,1)S(1)}, bf16[72,1152]{1,0:T(8,128)(2,1)S(1)}, u32[]{:S(2)}, u32[]{:S(2)}) %collective-permute-start.7) | collective-permute-done | bytes 165920 | tf_op jit(solution)/shard_map/ppermute | solution.py:890
  43.9 2.0 %collective-permute-start.10 = (bf16[144,1152]{1,0:T(8,128)(2,1)S(1)}, bf16[144,1152]{1,0:T(8,128)(2,1)S(1)}, u32[]{:S(2)}, u32[]{:S(2)}) collective-permute-start(bf16[144,1152]{1,0:T(8,128)(2,1)S(1)} %shard_map.121.refs_13_.refs_10_), channel_id=1, source_target_pairs={{0,16},{16,0},{1,17},{17,1},{2,18},{18,2},{3,19},{19,3},{4,20},{20... | collective-permute-start | bytes 995336 | tf_op jit(solution)/shard_map/ppermute | solution.py:776
  45.9 1.5 %collective-permute-start.8 = (bf16[576,256]{1,0:T(8,128)(2,1)S(1)}, bf16[576,256]{1,0:T(8,128)(2,1)S(1)}, u32[]{:S(2)}, u32[]{:S(2)}) collective-permute-start(bf16[576,256]{1,0:T(8,128)(2,1)S(1)} %shard_map.119), channel_id=1, source_target_pairs={{0,2},{2,0},{1,3},{3,1},{4,6},{6,4},{5,7},{7,5},{8,10},{10,8},{9,1... | collective-permute-start | bytes 884744 | tf_op jit(solution)/shard_map/ppermute | solution.py:776
  47.9 7.9 %collective-permute-done.8.refs_1_ = bf16[576,256]{1,0:T(8,128)(2,1)S(1)} collective-permute-done((bf16[576,256]{1,0:T(8,128)(2,1)S(1)}, bf16[576,256]{1,0:T(8,128)(2,1)S(1)}, u32[]{:S(2)}, u32[]{:S(2)}) %collective-permute-start.8) | collective-permute-done | bytes 294944 | tf_op jit(solution)/shard_map/ppermute | solution.py:776
  55.8 1.3 shard_map.122
  57.6 1.5 %collective-permute-start.18 = (bf16[72,1152]{1,0:T(8,128)(2,1)S(1)}, bf16[72,1152]{1,0:T(8,128)(2,1)S(1)}, u32[]{:S(2)}, u32[]{:S(2)}) collective-permute-start(bf16[72,1152]{1,0:T(8,128)(2,1)S(1)} %get-tuple-element.115), channel_id=1, source_target_pairs={{0,2},{2,0},{1,3},{3,1},{4,6},{6,4},{5,7},{7,5},{8,10},{10,8},{9,1... | collective-permute-start | bytes 497672 | tf_op jit(solution)/shard_map/ppermute | solution.py:776
  60.4 6.8 %collective-permute-done.20.refs_5_ = bf16[288,1152]{1,0:T(8,128)(2,1)S(1)} collective-permute-done((bf16[288,1152]{1,0:T(8,128)(2,1)S(1)}, bf16[288,1152]{1,0:T(8,128)(2,1)S(1)}, u32[]{:S(2)}, u32[]{:S(2)}) %collective-permute-start.20) | collective-permute-done | bytes 663584 | tf_op jit(solution)/shard_map/ppermute | solution.py:776
  67.8 3.8 %shard_map.118 = bf16[576,256]{1,0:T(8,128)(2,1)S(1)} custom-call(s32[3]{0:T(128)S(1)} %pad_add_fusion.info, bf16[3,8,80,256]{3,2,1,0:T(8,128)(2,1)S(1)} %shard_map.114.refs_2_.refs_0_.refs_4_, bf16[3,8,80,256]{3,2,1,0:T(8,128)(2,1)S(1)} %shard_map.116.refs_1_.refs_5_.refs_2_, bf16[3,8,80,256]{3,2,1,0:T(8,128)(2,1)S(1)} %get-tuple-element.80.refs_0_.refs_2_, ...), custom_call_target="tpu_custom_call" | custom-call | flops 2415919104 | bytes 6225920 | tf_op jit(solution)/shard_map/pallas_call | solution.py:161
  71.6 1.5 %collective-permute-start.5 = (bf16[576,256]{1,0:T(8,128)(2,1)S(1)}, bf16[576,256]{1,0:T(8,128)(2,1)S(1)}, u32[]{:S(2)}, u32[]{:S(2)}) collective-permute-start(bf16[576,256]{1,0:T(8,128)(2,1)S(1)} %shard_map.118), channel_id=1, source_target_pairs={{0,2},{2,0},{1,3},{3,1},{4,6},{6,4},{5,7},{7,5},{8,10},{10,8},{9,1... | collective-permute-start | bytes 884744 | tf_op jit(solution)/shard_map/ppermute | solution.py:776
  73.1 1.6 %collective-permute-start.19 = (bf16[72,1152]{1,0:T(8,128)(2,1)S(1)}, bf16[72,1152]{1,0:T(8,128)(2,1)S(1)}, u32[]{:S(2)}, u32[]{:S(2)}) collective-permute-start(bf16[72,1152]{1,0:T(8,128)(2,1)S(1)} %collective-permute-done.18.own), channel_id=1, source_target_pairs={{0,4},{4,0},{8,12},{12,8},{1,5},{5,1},{9,13},{13,9},{2,6},{6,2},{1... | collective-permute-start | bytes 497672 | tf_op jit(solution)/shard_map/ppermute | solution.py:890
  75.2 4.5 %collective-permute-done.19.other = bf16[72,1152]{1,0:T(8,128)(2,1)S(1)} collective-permute-done((bf16[72,1152]{1,0:T(8,128)(2,1)S(1)}, bf16[72,1152]{1,0:T(8,128)(2,1)S(1)}, u32[]{:S(2)}, u32[]{:S(2)}) %collective-permute-start.19) | collective-permute-done | bytes 165920 | tf_op jit(solution)/shard_map/ppermute | solution.py:890
  80.1 1.3 collective-permute-start.23
  81.4 3.9 %collective-permute-start.14 = (bf16[592,128]{1,0:T(8,128)(2,1)S(1)}, bf16[592,128]{1,0:T(8,128)(2,1)S(1)}, u32[]{:S(2)}, u32[]{:S(2)}) collective-permute-start(bf16[592,128]{1,0:T(8,128)(2,1)S(1)} %get-tuple-element.98), channel_id=1, source_target_pairs={{0,8},{4,12},{8,0},{12,4},{1,9},{5,13},{9,1},{13,5},{2,10},{6,14},... | collective-permute-start | bytes 454664 | tf_op jit(solution)/shard_map/ppermute | solution.py:977
  85.3 4.0 %shard_map.117.refs_0_ = bf16[576,256]{1,0:T(8,128)(2,1)S(1)} custom-call(s32[3]{0:T(128)S(1)} %pad_add_fusion.info, bf16[3,8,80,256]{3,2,1,0:T(8,128)(2,1)S(1)} %shard_map.114.refs_2_.refs_0_.refs_4_, bf16[3,8,80,256]{3,2,1,0:T(8,128)(2,1)S(1)} %shard_map.116.refs_1_.refs_5_.refs_2_, bf16[3,8,80,256]{3,2,1,0:T(8,128)(2,1)S(1)} %get-tuple-element.80.refs_0_.refs_2_, ...), custom_call_target="tpu_custom_call" | custom-call | flops 2415919104 | bytes 6225920 | tf_op jit(solution)/shard_map/pallas_call | solution.py:161
  89.3 4.9 %collective-permute-start.15 = (bf16[592,128]{1,0:T(8,128)(2,1)S(1)}, bf16[592,128]{1,0:T(8,128)(2,1)S(1)}, u32[]{:S(2)}, u32[]{:S(2)}) collective-permute-start(bf16[592,128]{1,0:T(8,128)(2,1)S(1)} %get-tuple-element.106), channel_id=1, source_target_pairs={{0,12},{4,8},{8,4},{12,0},{1,13},{5,9},{9,5},{13,1},{2,14},{6,10},... | collective-permute-start | bytes 454664 | tf_op jit(solution)/shard_map/ppermute | solution.py:977
  94.1 1.7 %shard_map.123 = (bf16[592,128]{1,0:T(8,128)(2,1)S(1)}, bf16[592,128]{1,0:T(8,128)(2,1)S(1)}, bf16[576,128]{1,0:T(8,128)(2,1)S(1)}, bf16[576,128]{1,0:T(8,128)(2,1)S(1)}) custom-call(s32[3]{0:T(128)S(1)} %pad_add_fusion.info, bf16[576,256]{1,0:T(8,128)(2,1)S(1)} %shard_map.117.refs_0_, bf16[576,256]{1,0:T(8,128)(2,1)S(1)} %collective-permute-done.5.refs_1_, ...), custom_call_target="tpu_custom_call" | custom-call | flops 679477248 | bytes 6193152 | tf_op jit(solution)/shard_map/pallas_call | solution.py:161
  97.6 6.6 %collective-permute-done.17.refs_3_ = bf16[576,128]{1,0:T(8,128)(2,1)S(1)} collective-permute-done((bf16[576,128]{1,0:T(8,128)(2,1)S(1)}, bf16[576,128]{1,0:T(8,128)(2,1)S(1)}, u32[]{:S(2)}, u32[]{:S(2)}) %collective-permute-start.17) | collective-permute-done | bytes 147488 | tf_op jit(solution)/shard_map/ppermute | solution.py:977
  104.9 4.4 %collective-permute-done.13.refs_3_ = bf16[576,128]{1,0:T(8,128)(2,1)S(1)} collective-permute-done((bf16[576,128]{1,0:T(8,128)(2,1)S(1)}, bf16[576,128]{1,0:T(8,128)(2,1)S(1)}, u32[]{:S(2)}, u32[]{:S(2)}) %collective-permute-start.13) | collective-permute-done | bytes 147488 | tf_op jit(solution)/shard_map/ppermute | solution.py:977
  110.1 4.5 %collective-permute-done.12.refs_1_ = bf16[592,128]{1,0:T(8,128)(2,1)S(1)} collective-permute-done((bf16[592,128]{1,0:T(8,128)(2,1)S(1)}, bf16[592,128]{1,0:T(8,128)(2,1)S(1)}, u32[]{:S(2)}, u32[]{:S(2)}) %collective-permute-start.12) | collective-permute-done | bytes 151584 | tf_op jit(solution)/shard_map/ppermute | solution.py:977
  115.1 2.2 %shard_map.125 = (bf16[1152,256]{1,0:T(8,128)(2,1)S(1)}, f32[8,256]{1,0:T(8,128)S(1)}, bf16[3,576,256]{2,1,0:T(8,128)(2,1)S(1)}) custom-call(s32[3]{0:T(128)S(1)} %pad_add_fusion.info, bf16[592,128]{1,0:T(8,128)(2,1)S(1)} %collective-permute-done.14.refs_0_, bf16[592,128]{1,0:T(8,128)(2,1)S(1)} %collective-permute-done.15.refs_1_, ...), custom_call_target="tpu_custom_call" | custom-call | flops 1019215872 | bytes 4588544 | tf_op jit(solution)/shard_map/pallas_call | solution.py:161
  117.3 2.8 %shard_map.126 = (bf16[1152,256]{1,0:T(8,128)(2,1)S(1)}, f32[8,256]{1,0:T(8,128)S(1)}, bf16[576,512]{1,0:T(8,128)(2,1)S(1)}) custom-call(s32[3]{0:T(128)S(1)} %pad_add_fusion.info, bf16[592,128]{1,0:T(8,128)(2,1)S(1)} %get-tuple-element.102.refs_0_, bf16[592,128]{1,0:T(8,128)(2,1)S(1)} %collective-permute-done.12.refs_1_, ...), custom_call_target="tpu_custom_call" | custom-call | flops 1019215872 | bytes 5473280 | tf_op jit(solution)/shard_map/pallas_call | solution.py:161
  120.2 3.6 %shard_map.128.refs_5_ = bf16[576,512]{1,0:T(8,128)(2,1)S(1)} custom-call(s32[3]{0:T(128)S(1)} %pad_add_fusion.info, bf16[1152,256]{1,0:T(8,128)(2,1)S(1)} %get-tuple-element.111.refs_0_, f32[8,256]{1,0:T(8,128)S(1)} %get-tuple-element.112.refs_1_, bf16[1152,256]{1,0:T(8,128)(2,1)S(1)} %get-tuple-element.113.refs_2_, ...), custom_call_target="tpu_custom_call" | custom-call | flops 2038431744 | bytes 5177344 | tf_op jit(solution)/shard_map/pallas_call | solution.py:161
  123.8 1.6 %shard_map.129 = (bf16[2,2,288,128]{3,2,1,0:T(8,128)(2,1)S(1)}, bf16[2,2,288,128]{3,2,1,0:T(8,128)(2,1)S(1)}, f32[2,128]{1,0:T(2,128)S(1)}) custom-call(s32[3]{0:T(128)S(1)} %pad_add_fusion.info, bf16[592,128]{1,0:T(8,128)(2,1)S(1)} %get-tuple-element.102.refs_0_, bf16[592,128]{1,0:T(8,128)(2,1)S(1)} %collective-permute-done.12.refs_1_, ...), custom_call_target="tpu_custom_call" | custom-call | flops 679477248 | bytes 4431872 | tf_op jit(solution)/shard_map/pallas_call | solution.py:161
  127.2 1.2 shard_map.131
  129.1 2.5 %collective-permute-start.38 = (bf16[288,128]{1,0:T(8,128)(2,1)S(1)}, bf16[288,128]{1,0:T(8,128)(2,1)S(1)}, u32[]{:S(2)}, u32[]{:S(2)}) collective-permute-start(bf16[288,128]{1,0:T(8,128)(2,1)S(1)} %get-tuple-element.144), channel_id=1, source_target_pairs={{0,10},{2,8},{4,14},{6,12},{8,2},{10,0},{12,6},{14,4},{1,11},{3,9}... | collective-permute-start | bytes 221192 | tf_op jit(solution)/shard_map/ppermute | solution.py:1046
  131.6 1.5 %collective-permute-start.40 = (bf16[288,128]{1,0:T(8,128)(2,1)S(1)}, bf16[288,128]{1,0:T(8,128)(2,1)S(1)}, u32[]{:S(2)}, u32[]{:S(2)}) collective-permute-start(bf16[288,128]{1,0:T(8,128)(2,1)S(1)} %get-tuple-element.146), channel_id=1, source_target_pairs={{0,14},{2,12},{4,10},{6,8},{8,6},{10,4},{12,2},{14,0},{1,15},{3,13... | collective-permute-start | bytes 221192 | tf_op jit(solution)/shard_map/ppermute | solution.py:1046
  135.0 2.1 %collective-permute-start.39 = (bf16[288,128]{1,0:T(8,128)(2,1)S(1)}, bf16[288,128]{1,0:T(8,128)(2,1)S(1)}, u32[]{:S(2)}, u32[]{:S(2)}) collective-permute-start(bf16[288,128]{1,0:T(8,128)(2,1)S(1)} %get-tuple-element.145), channel_id=1, source_target_pairs={{0,12},{2,14},{4,8},{6,10},{8,4},{10,6},{12,0},{14,2},{1,13},{3,15... | collective-permute-start | bytes 221192 | tf_op jit(solution)/shard_map/ppermute | solution.py:1046
  138.5 3.8 %collective-permute-done.38.refs_5_ = bf16[288,128]{1,0:T(8,128)(2,1)S(1)} collective-permute-done((bf16[288,128]{1,0:T(8,128)(2,1)S(1)}, bf16[288,128]{1,0:T(8,128)(2,1)S(1)}, u32[]{:S(2)}, u32[]{:S(2)}) %collective-permute-start.38) | collective-permute-done | bytes 73760 | tf_op jit(solution)/shard_map/ppermute | solution.py:1046
  142.2 2.1 %collective-permute-start.34 = (bf16[288,128]{1,0:T(8,128)(2,1)S(1)}, bf16[288,128]{1,0:T(8,128)(2,1)S(1)}, u32[]{:S(2)}, u32[]{:S(2)}) collective-permute-start(bf16[288,128]{1,0:T(8,128)(2,1)S(1)} %get-tuple-element.136), channel_id=1, source_target_pairs={{0,6},{2,4},{4,2},{6,0},{8,14},{10,12},{12,10},{14,8},{1,7},{3,5},... | collective-permute-start | bytes 221192 | tf_op jit(solution)/shard_map/ppermute | solution.py:1046
  144.4 2.1 %collective-permute-done.33.refs_2_ = bf16[288,128]{1,0:T(8,128)(2,1)S(1)} collective-permute-done((bf16[288,128]{1,0:T(8,128)(2,1)S(1)}, bf16[288,128]{1,0:T(8,128)(2,1)S(1)}, u32[]{:S(2)}, u32[]{:S(2)}) %collective-permute-start.33) | collective-permute-done | bytes 73760 | tf_op jit(solution)/shard_map/ppermute | solution.py:1046
  (71 shorter events, 16.7 us)
Async XLA Ops:
  1.3 16.1 %collective-permute-start.2 = (bf16[576,256]{1,0:T(8,128)(2,1)S(1)}, bf16[576,256]{1,0:T(8,128)(2,1)S(1)}, u32[]{:S(2)}, u32[]{:S(2)}) collective-permute-start(bf16[576,256]{1,0:T(8,128)(2,1)S(1)} %get-tuple-element.77.refs_2_), channel_id=1, source_target_pairs={{0,2},{2,0},{1,3},{3,1},{4,6},{6,4},{5,7},{7,5},{8,10},{10,8},{9,1... | collective-permute-start | bytes 884744 | tf_op jit(solution)/shard_map/ppermute | solution.py:776
  4.3 11.0 %collective-permute-start.1 = (bf16[576,128]{1,0:T(8,128)(2,1)}, bf16[576,128]{1,0:T(8,128)(2,1)S(1)}, u32[]{:S(2)}, u32[]{:S(2)}) collective-permute-start(bf16[576,128]{1,0:T(8,128)(2,1)} %bitcast.7), channel_id=1, source_target_pairs={{0,2},{2,0},{1,3},{3,1},{4,6},{6,4},{5,7},{7,5},{8,10},{10,8},{9,1... | collective-permute-start | bytes 442376 | tf_op jit(solution)/shard_map/ppermute | solution.py:776
  4.4 17.3 %collective-permute-start.3 = (bf16[576,256]{1,0:T(8,128)(2,1)S(1)}, bf16[576,256]{1,0:T(8,128)(2,1)S(1)}, u32[]{:S(2)}, u32[]{:S(2)}) collective-permute-start(bf16[576,256]{1,0:T(8,128)(2,1)S(1)} %get-tuple-element.81.refs_0_.refs_3_), channel_id=1, source_target_pairs={{0,2},{2,0},{1,3},{3,1},{4,6},{6,4},{5,7},{7,5},{8,10},{10,8},{9,1... | collective-permute-start | bytes 884744 | tf_op jit(solution)/shard_map/ppermute | solution.py:776
  6.3 21.6 %collective-permute-start = (bf16[576,256]{1,0:T(8,128)(2,1)S(1)}, bf16[576,256]{1,0:T(8,128)(2,1)S(1)}, u32[]{:S(2)}, u32[]{:S(2)}) collective-permute-start(bf16[576,256]{1,0:T(8,128)(2,1)S(1)} %get-tuple-element.76.refs_0_.refs_2_), channel_id=1, source_target_pairs={{0,2},{2,0},{1,3},{3,1},{4,6},{6,4},{5,7},{7,5},{8,10},{10,8},{9,1... | collective-permute-start | bytes 884744 | tf_op jit(solution)/shard_map/ppermute | solution.py:776
  6.4 27.9 %collective-permute-start.4 = (bf16[576,256]{1,0:T(8,128)(2,1)S(1)}, bf16[576,256]{1,0:T(8,128)(2,1)S(1)}, u32[]{:S(2)}, u32[]{:S(2)}) collective-permute-start(bf16[576,256]{1,0:T(8,128)(2,1)S(1)} %get-tuple-element.86.refs_0_.refs_3_), channel_id=1, source_target_pairs={{0,2},{2,0},{1,3},{3,1},{4,6},{6,4},{5,7},{7,5},{8,10},{10,8},{9,1... | collective-permute-start | bytes 884744 | tf_op jit(solution)/shard_map/ppermute | solution.py:776
  11.0 6.3 %copy-start.3 = (bf16[1,1,576,128]{3,2,1,0:T(8,128)(2,1)S(1)}, bf16[1,1,576,128]{3,2,1,0:T(8,128)(2,1)}, u32[]{:S(2)}) copy-start(bf16[1,1,576,128]{3,2,1,0:T(8,128)(2,1)} %param.12) | copy-start | bytes 442372
  15.3 22.6 %collective-permute-start.6 = (bf16[72,1152]{1,0:T(8,128)(2,1)S(1)}, bf16[72,1152]{1,0:T(8,128)(2,1)S(1)}, u32[]{:S(2)}, u32[]{:S(2)}) collective-permute-start(bf16[72,1152]{1,0:T(8,128)(2,1)S(1)} %get-tuple-element.92), channel_id=1, source_target_pairs={{0,2},{2,0},{1,3},{3,1},{4,6},{6,4},{5,7},{7,5},{8,10},{10,8},{9,1... | collective-permute-start | bytes 497672 | tf_op jit(solution)/shard_map/ppermute | solution.py:776
  38.0 5.5 %collective-permute-start.7 = (bf16[72,1152]{1,0:T(8,128)(2,1)S(1)}, bf16[72,1152]{1,0:T(8,128)(2,1)S(1)}, u32[]{:S(2)}, u32[]{:S(2)}) collective-permute-start(bf16[72,1152]{1,0:T(8,128)(2,1)S(1)} %collective-permute-done.6.own), channel_id=1, source_target_pairs={{0,4},{4,0},{8,12},{12,8},{1,5},{5,1},{9,13},{13,9},{2,6},{6,2},{1... | collective-permute-start | bytes 497672 | tf_op jit(solution)/shard_map/ppermute | solution.py:890
  40.1 15.7 %copy-start.1 = (bf16[576,1152]{1,0:T(8,128)(2,1)S(1)}, bf16[576,1152]{1,0:T(8,128)(2,1)}, u32[]{:S(2)}) copy-start(bf16[576,1152]{1,0:T(8,128)(2,1)} %refs_12_.1) | copy-start | bytes 3981316
  43.9 13.3 %collective-permute-start.10 = (bf16[144,1152]{1,0:T(8,128)(2,1)S(1)}, bf16[144,1152]{1,0:T(8,128)(2,1)S(1)}, u32[]{:S(2)}, u32[]{:S(2)}) collective-permute-start(bf16[144,1152]{1,0:T(8,128)(2,1)S(1)} %shard_map.121.refs_13_.refs_10_), channel_id=1, source_target_pairs={{0,16},{16,0},{1,17},{17,1},{2,18},{18,2},{3,19},{19,3},{4,20},{20... | collective-permute-start | bytes 995336 | tf_op jit(solution)/shard_map/ppermute | solution.py:776
  45.9 9.9 %collective-permute-start.8 = (bf16[576,256]{1,0:T(8,128)(2,1)S(1)}, bf16[576,256]{1,0:T(8,128)(2,1)S(1)}, u32[]{:S(2)}, u32[]{:S(2)}) collective-permute-start(bf16[576,256]{1,0:T(8,128)(2,1)S(1)} %shard_map.119), channel_id=1, source_target_pairs={{0,2},{2,0},{1,3},{3,1},{4,6},{6,4},{5,7},{7,5},{8,10},{10,8},{9,1... | collective-permute-start | bytes 884744 | tf_op jit(solution)/shard_map/ppermute | solution.py:776
  47.4 19.8 %collective-permute-start.20 = (bf16[288,1152]{1,0:T(8,128)(2,1)S(1)}, bf16[288,1152]{1,0:T(8,128)(2,1)S(1)}, u32[]{:S(2)}, u32[]{:S(2)}) collective-permute-start(bf16[288,1152]{1,0:T(8,128)(2,1)S(1)} %get-tuple-element.119), channel_id=1, source_target_pairs={{0,2},{2,0},{1,3},{3,1},{4,6},{6,4},{5,7},{7,5},{8,10},{10,8},{9,1... | collective-permute-start | bytes 1990664 | tf_op jit(solution)/shard_map/ppermute | solution.py:776
  57.0 2.1 %collective-permute-start.9 = (bf16[144,1152]{1,0:T(8,128)(2,1)S(1)}, bf16[144,1152]{1,0:T(8,128)(2,1)S(1)}, u32[]{:S(2)}, u32[]{:S(2)}) collective-permute-start(bf16[144,1152]{1,0:T(8,128)(2,1)S(1)} %shard_map.121.refs_13_.refs_10_), channel_id=1, source_target_pairs={{0,1},{1,0},{2,3},{3,2},{4,5},{5,4},{6,7},{7,6},{8,9},{9,8},{10,11... | collective-permute-start | bytes 995336 | tf_op jit(solution)/shard_map/ppermute | solution.py:776
  57.1 2.1 %collective-permute-start.11 = (bf16[144,1152]{1,0:T(8,128)(2,1)S(1)}, bf16[144,1152]{1,0:T(8,128)(2,1)S(1)}, u32[]{:S(2)}, u32[]{:S(2)}) collective-permute-start(bf16[144,1152]{1,0:T(8,128)(2,1)S(1)} %collective-permute-done.10.refs_15_.refs_12_), channel_id=1, source_target_pairs={{0,1},{1,0},{2,3},{3,2},{4,5},{5,4},{6,7},{7,6},{8,9},{9,8},{10,11... | collective-permute-start | bytes 995336 | tf_op jit(solution)/shard_map/ppermute | solution.py:776
  57.6 15.5 %collective-permute-start.18 = (bf16[72,1152]{1,0:T(8,128)(2,1)S(1)}, bf16[72,1152]{1,0:T(8,128)(2,1)S(1)}, u32[]{:S(2)}, u32[]{:S(2)}) collective-permute-start(bf16[72,1152]{1,0:T(8,128)(2,1)S(1)} %get-tuple-element.115), channel_id=1, source_target_pairs={{0,2},{2,0},{1,3},{3,1},{4,6},{6,4},{5,7},{7,5},{8,10},{10,8},{9,1... | collective-permute-start | bytes 497672 | tf_op jit(solution)/shard_map/ppermute | solution.py:776
  67.2 28.7 %collective-permute-start.24 = (bf16[288,1152]{1,0:T(8,128)(2,1)S(1)}, bf16[288,1152]{1,0:T(8,128)(2,1)S(1)}, u32[]{:S(2)}, u32[]{:S(2)}) collective-permute-start(bf16[288,1152]{1,0:T(8,128)(2,1)S(1)} %collective-permute-done.20.refs_5_), channel_id=1, source_target_pairs={{0,16},{16,0},{1,17},{17,1},{2,18},{18,2},{3,19},{19,3},{4,20},{20... | collective-permute-start | bytes 1990664 | tf_op jit(solution)/shard_map/ppermute | solution.py:776
  71.6 13.7 %collective-permute-start.5 = (bf16[576,256]{1,0:T(8,128)(2,1)S(1)}, bf16[576,256]{1,0:T(8,128)(2,1)S(1)}, u32[]{:S(2)}, u32[]{:S(2)}) collective-permute-start(bf16[576,256]{1,0:T(8,128)(2,1)S(1)} %shard_map.118), channel_id=1, source_target_pairs={{0,2},{2,0},{1,3},{3,1},{4,6},{6,4},{5,7},{7,5},{8,10},{10,8},{9,1... | collective-permute-start | bytes 884744 | tf_op jit(solution)/shard_map/ppermute | solution.py:776
  73.1 6.6 %collective-permute-start.19 = (bf16[72,1152]{1,0:T(8,128)(2,1)S(1)}, bf16[72,1152]{1,0:T(8,128)(2,1)S(1)}, u32[]{:S(2)}, u32[]{:S(2)}) collective-permute-start(bf16[72,1152]{1,0:T(8,128)(2,1)S(1)} %collective-permute-done.18.own), channel_id=1, source_target_pairs={{0,4},{4,0},{8,12},{12,8},{1,5},{5,1},{9,13},{13,9},{2,6},{6,2},{1... | collective-permute-start | bytes 497672 | tf_op jit(solution)/shard_map/ppermute | solution.py:890
  74.7 14.6 %collective-permute-start.27 = (bf16[144,1152]{1,0:T(8,128)(2,1)S(1)}, bf16[144,1152]{1,0:T(8,128)(2,1)S(1)}, u32[]{:S(2)}, u32[]{:S(2)}) collective-permute-start(bf16[144,1152]{1,0:T(8,128)(2,1)S(1)} %get-tuple-element.127), channel_id=1, source_target_pairs={{0,2},{2,0},{1,3},{3,1},{4,6},{6,4},{5,7},{7,5},{8,10},{10,8},{9,1... | collective-permute-start | bytes 995336 | tf_op jit(solution)/shard_map/ppermute | solution.py:776
  80.1 16.4 %collective-permute-start.23 = (bf16[144,1152]{1,0:T(8,128)(2,1)S(1)}, bf16[144,1152]{1,0:T(8,128)(2,1)S(1)}, u32[]{:S(2)}, u32[]{:S(2)}) collective-permute-start(bf16[144,1152]{1,0:T(8,128)(2,1)S(1)} %shard_map.127.refs_4_), channel_id=1, source_target_pairs={{0,16},{16,0},{1,17},{17,1},{2,18},{18,2},{3,19},{19,3},{4,20},{20... | collective-permute-start | bytes 995336 | tf_op jit(solution)/shard_map/ppermute | solution.py:776
  81.4 14.7 %collective-permute-start.14 = (bf16[592,128]{1,0:T(8,128)(2,1)S(1)}, bf16[592,128]{1,0:T(8,128)(2,1)S(1)}, u32[]{:S(2)}, u32[]{:S(2)}) collective-permute-start(bf16[592,128]{1,0:T(8,128)(2,1)S(1)} %get-tuple-element.98), channel_id=1, source_target_pairs={{0,8},{4,12},{8,0},{12,4},{1,9},{5,13},{9,1},{13,5},{2,10},{6,14},... | collective-permute-start | bytes 454664 | tf_op jit(solution)/shard_map/ppermute | solution.py:977
  85.2 10.6 %collective-permute-start.16 = (bf16[576,128]{1,0:T(8,128)(2,1)S(1)}, bf16[576,128]{1,0:T(8,128)(2,1)S(1)}, u32[]{:S(2)}, u32[]{:S(2)}) collective-permute-start(bf16[576,128]{1,0:T(8,128)(2,1)S(1)} %get-tuple-element.107), channel_id=1, source_target_pairs={{0,8},{4,12},{8,0},{12,4},{1,9},{5,13},{9,1},{13,5},{2,10},{6,14},... | collective-permute-start | bytes 442376 | tf_op jit(solution)/shard_map/ppermute | solution.py:977
  89.3 8.3 %collective-permute-start.15 = (bf16[592,128]{1,0:T(8,128)(2,1)S(1)}, bf16[592,128]{1,0:T(8,128)(2,1)S(1)}, u32[]{:S(2)}, u32[]{:S(2)}) collective-permute-start(bf16[592,128]{1,0:T(8,128)(2,1)S(1)} %get-tuple-element.106), channel_id=1, source_target_pairs={{0,12},{4,8},{8,4},{12,0},{1,13},{5,9},{9,5},{13,1},{2,14},{6,10},... | collective-permute-start | bytes 454664 | tf_op jit(solution)/shard_map/ppermute | solution.py:977
  94.1 20.9 %copy-start = (bf16[3,576,1152]{2,1,0:T(8,128)(2,1)S(1)}, bf16[3,576,1152]{2,1,0:T(8,128)(2,1)}, u32[]{:S(2)}) copy-start(bf16[3,576,1152]{2,1,0:T(8,128)(2,1)} %refs_5_.3) | copy-start | bytes 11943940
  95.8 24.3 %collective-permute-start.22 = (bf16[288,1152]{1,0:T(8,128)(2,1)S(1)}, bf16[288,1152]{1,0:T(8,128)(2,1)S(1)}, u32[]{:S(2)}, u32[]{:S(2)}) collective-permute-start(bf16[288,1152]{1,0:T(8,128)(2,1)S(1)} %collective-permute-done.20.refs_5_), channel_id=1, source_target_pairs={{0,1},{1,0},{2,3},{3,2},{4,5},{5,4},{6,7},{7,6},{8,9},{9,8},{10,11... | collective-permute-start | bytes 1990664 | tf_op jit(solution)/shard_map/ppermute | solution.py:776
  95.9 14.2 %collective-permute-start.29 = (bf16[144,1152]{1,0:T(8,128)(2,1)S(1)}, bf16[144,1152]{1,0:T(8,128)(2,1)S(1)}, u32[]{:S(2)}, u32[]{:S(2)}) collective-permute-start(bf16[144,1152]{1,0:T(8,128)(2,1)S(1)} %collective-permute-done.27.refs_7_.refs_6_), channel_id=1, source_target_pairs={{0,16},{16,0},{1,17},{17,1},{2,18},{18,2},{3,19},{19,3},{4,20},{20... | collective-permute-start | bytes 995336 | tf_op jit(solution)/shard_map/ppermute | solution.py:776
  96.0 24.1 %collective-permute-start.26 = (bf16[288,1152]{1,0:T(8,128)(2,1)S(1)}, bf16[288,1152]{1,0:T(8,128)(2,1)S(1)}, u32[]{:S(2)}, u32[]{:S(2)}) collective-permute-start(bf16[288,1152]{1,0:T(8,128)(2,1)S(1)} %collective-permute-done.24.refs_9_), channel_id=1, source_target_pairs={{0,1},{1,0},{2,3},{3,2},{4,5},{5,4},{6,7},{7,6},{8,9},{9,8},{10,11... | collective-permute-start | bytes 1990664 | tf_op jit(solution)/shard_map/ppermute | solution.py:776
  96.5 7.8 %collective-permute-start.17 = (bf16[576,128]{1,0:T(8,128)(2,1)S(1)}, bf16[576,128]{1,0:T(8,128)(2,1)S(1)}, u32[]{:S(2)}, u32[]{:S(2)}) collective-permute-start(bf16[576,128]{1,0:T(8,128)(2,1)S(1)} %get-tuple-element.108), channel_id=1, source_target_pairs={{0,12},{4,8},{8,4},{12,0},{1,13},{5,9},{9,5},{13,1},{2,14},{6,10},... | collective-permute-start | bytes 442376 | tf_op jit(solution)/shard_map/ppermute | solution.py:977
  97.6 17.0 %collective-permute-start.25 = (bf16[144,1152]{1,0:T(8,128)(2,1)S(1)}, bf16[144,1152]{1,0:T(8,128)(2,1)S(1)}, u32[]{:S(2)}, u32[]{:S(2)}) collective-permute-start(bf16[144,1152]{1,0:T(8,128)(2,1)S(1)} %collective-permute-done.23.refs_8_), channel_id=1, source_target_pairs={{0,1},{1,0},{2,3},{3,2},{4,5},{5,4},{6,7},{7,6},{8,9},{9,8},{10,11... | collective-permute-start | bytes 995336 | tf_op jit(solution)/shard_map/ppermute | solution.py:776
  104.2 5.1 %collective-permute-start.13 = (bf16[576,128]{1,0:T(8,128)(2,1)S(1)}, bf16[576,128]{1,0:T(8,128)(2,1)S(1)}, u32[]{:S(2)}, u32[]{:S(2)}) collective-permute-start(bf16[576,128]{1,0:T(8,128)(2,1)S(1)} %get-tuple-element.105), channel_id=1, source_target_pairs={{0,4},{4,0},{8,12},{12,8},{1,5},{5,1},{9,13},{13,9},{2,6},{6,2},{1... | collective-permute-start | bytes 442376 | tf_op jit(solution)/shard_map/ppermute | solution.py:977
  109.4 5.2 %collective-permute-start.12 = (bf16[592,128]{1,0:T(8,128)(2,1)S(1)}, bf16[592,128]{1,0:T(8,128)(2,1)S(1)}, u32[]{:S(2)}, u32[]{:S(2)}) collective-permute-start(bf16[592,128]{1,0:T(8,128)(2,1)S(1)} %get-tuple-element.103), channel_id=1, source_target_pairs={{0,4},{4,0},{8,12},{12,8},{1,5},{5,1},{9,13},{13,9},{2,6},{6,2},{1... | collective-permute-start | bytes 454664 | tf_op jit(solution)/shard_map/ppermute | solution.py:977
  110.1 10.1 %collective-permute-start.21 = (bf16[144,1152]{1,0:T(8,128)(2,1)S(1)}, bf16[144,1152]{1,0:T(8,128)(2,1)S(1)}, u32[]{:S(2)}, u32[]{:S(2)}) collective-permute-start(bf16[144,1152]{1,0:T(8,128)(2,1)S(1)} %shard_map.127.refs_4_), channel_id=1, source_target_pairs={{0,1},{1,0},{2,3},{3,2},{4,5},{5,4},{6,7},{7,6},{8,9},{9,8},{10,11... | collective-permute-start | bytes 995336 | tf_op jit(solution)/shard_map/ppermute | solution.py:776
  114.6 9.2 %collective-permute-start.28 = (bf16[144,1152]{1,0:T(8,128)(2,1)S(1)}, bf16[144,1152]{1,0:T(8,128)(2,1)S(1)}, u32[]{:S(2)}, u32[]{:S(2)}) collective-permute-start(bf16[144,1152]{1,0:T(8,128)(2,1)S(1)} %collective-permute-done.27.refs_7_.refs_6_), channel_id=1, source_target_pairs={{0,1},{1,0},{2,3},{3,2},{4,5},{5,4},{6,7},{7,6},{8,9},{9,8},{10,11... | collective-permute-start | bytes 995336 | tf_op jit(solution)/shard_map/ppermute | solution.py:776
  114.6 9.2 %collective-permute-start.30 = (bf16[144,1152]{1,0:T(8,128)(2,1)S(1)}, bf16[144,1152]{1,0:T(8,128)(2,1)S(1)}, u32[]{:S(2)}, u32[]{:S(2)}) collective-permute-start(bf16[144,1152]{1,0:T(8,128)(2,1)S(1)} %collective-permute-done.29.refs_9_.refs_8_), channel_id=1, source_target_pairs={{0,1},{1,0},{2,3},{3,2},{4,5},{5,4},{6,7},{7,6},{8,9},{9,8},{10,11... | collective-permute-start | bytes 995336 | tf_op jit(solution)/shard_map/ppermute | solution.py:776
  120.2 3.6 %copy-start.2 = (bf16[576,1152]{1,0:T(8,128)(2,1)S(1)}, bf16[576,1152]{1,0:T(8,128)(2,1)}, u32[]{:S(2)}) copy-start(bf16[576,1152]{1,0:T(8,128)(2,1)} %refs_6_.3) | copy-start | bytes 3981316
  125.4 11.8 %collective-permute-start.31 = (bf16[2,2,288,128]{3,2,1,0:T(8,128)(2,1)S(1)}, bf16[2,2,288,128]{3,2,1,0:T(8,128)(2,1)S(1)}, u32[]{:S(2)}, u32[]{:S(2)}) collective-permute-start(bf16[2,2,288,128]{3,2,1,0:T(8,128)(2,1)S(1)} %get-tuple-element.131), channel_id=1, source_target_pairs={{0,1},{1,0},{2,3},{3,2},{4,5},{5,4},{6,7},{7,6},{8,9},{9,8},{10,11... | collective-permute-start | bytes 884744 | tf_op jit(solution)/shard_map/ppermute | solution.py:776
  126.6 1.9 %collective-permute-start.37 = (bf16[2,1,288,128]{3,2,1,0:T(8,128)(2,1)S(1)}, bf16[2,1,288,128]{3,2,1,0:T(8,128)(2,1)S(1)}, u32[]{:S(2)}, u32[]{:S(2)}) collective-permute-start(bf16[2,1,288,128]{3,2,1,0:T(8,128)(2,1)S(1)} %get-tuple-element.142), channel_id=1, source_target_pairs={{0,1},{1,0},{2,3},{3,2},{4,5},{5,4},{6,7},{7,6},{8,9},{9,8},{10,11... | collective-permute-start | bytes 442376 | tf_op jit(solution)/shard_map/ppermute | solution.py:776
  128.4 4.8 %collective-permute-start.35 = (bf16[2,1,288,128]{3,2,1,0:T(8,128)(2,1)S(1)}, bf16[2,1,288,128]{3,2,1,0:T(8,128)(2,1)S(1)}, u32[]{:S(2)}, u32[]{:S(2)}) collective-permute-start(bf16[2,1,288,128]{3,2,1,0:T(8,128)(2,1)S(1)} %get-tuple-element.138), channel_id=1, source_target_pairs={{0,1},{1,0},{2,3},{3,2},{4,5},{5,4},{6,7},{7,6},{8,9},{9,8},{10,11... | collective-permute-start | bytes 442376 | tf_op jit(solution)/shard_map/ppermute | solution.py:776
  129.1 13.1 %collective-permute-start.38 = (bf16[288,128]{1,0:T(8,128)(2,1)S(1)}, bf16[288,128]{1,0:T(8,128)(2,1)S(1)}, u32[]{:S(2)}, u32[]{:S(2)}) collective-permute-start(bf16[288,128]{1,0:T(8,128)(2,1)S(1)} %get-tuple-element.144), channel_id=1, source_target_pairs={{0,10},{2,8},{4,14},{6,12},{8,2},{10,0},{12,6},{14,4},{1,11},{3,9}... | collective-permute-start | bytes 221192 | tf_op jit(solution)/shard_map/ppermute | solution.py:1046
  131.6 10.6 %collective-permute-start.40 = (bf16[288,128]{1,0:T(8,128)(2,1)S(1)}, bf16[288,128]{1,0:T(8,128)(2,1)S(1)}, u32[]{:S(2)}, u32[]{:S(2)}) collective-permute-start(bf16[288,128]{1,0:T(8,128)(2,1)S(1)} %get-tuple-element.146), channel_id=1, source_target_pairs={{0,14},{2,12},{4,10},{6,8},{8,6},{10,4},{12,2},{14,0},{1,15},{3,13... | collective-permute-start | bytes 221192 | tf_op jit(solution)/shard_map/ppermute | solution.py:1046
  133.8 10.6 %collective-permute-start.36 = (bf16[288,128]{1,0:T(8,128)(2,1)S(1)}, bf16[288,128]{1,0:T(8,128)(2,1)S(1)}, u32[]{:S(2)}, u32[]{:S(2)}) collective-permute-start(bf16[288,128]{1,0:T(8,128)(2,1)S(1)} %get-tuple-element.140), channel_id=1, source_target_pairs={{0,8},{2,10},{4,12},{6,14},{8,0},{10,2},{12,4},{14,6},{1,9},{3,11}... | collective-permute-start | bytes 221192 | tf_op jit(solution)/shard_map/ppermute | solution.py:1046
  135.0 9.5 %collective-permute-start.39 = (bf16[288,128]{1,0:T(8,128)(2,1)S(1)}, bf16[288,128]{1,0:T(8,128)(2,1)S(1)}, u32[]{:S(2)}, u32[]{:S(2)}) collective-permute-start(bf16[288,128]{1,0:T(8,128)(2,1)S(1)} %get-tuple-element.145), channel_id=1, source_target_pairs={{0,12},{2,14},{4,8},{6,10},{8,4},{10,6},{12,0},{14,2},{1,13},{3,15... | collective-permute-start | bytes 221192 | tf_op jit(solution)/shard_map/ppermute | solution.py:1046
  137.8 6.6 %collective-permute-start.32 = (bf16[288,128]{1,0:T(8,128)(2,1)S(1)}, bf16[288,128]{1,0:T(8,128)(2,1)S(1)}, u32[]{:S(2)}, u32[]{:S(2)}) collective-permute-start(bf16[288,128]{1,0:T(8,128)(2,1)S(1)} %get-tuple-element.134), channel_id=1, source_target_pairs={{0,2},{2,0},{4,6},{6,4},{8,10},{10,8},{12,14},{14,12},{1,3},{3,1},... | collective-permute-start | bytes 221192 | tf_op jit(solution)/shard_map/ppermute | solution.py:1046
  142.2 4.4 %collective-permute-start.33 = (bf16[288,128]{1,0:T(8,128)(2,1)S(1)}, bf16[288,128]{1,0:T(8,128)(2,1)S(1)}, u32[]{:S(2)}, u32[]{:S(2)}) collective-permute-start(bf16[288,128]{1,0:T(8,128)(2,1)S(1)} %get-tuple-element.135), channel_id=1, source_target_pairs={{0,4},{2,6},{4,0},{6,2},{8,12},{10,14},{12,8},{14,10},{1,5},{3,7},... | collective-permute-start | bytes 221192 | tf_op jit(solution)/shard_map/ppermute | solution.py:1046
  142.2 5.3 %collective-permute-start.34 = (bf16[288,128]{1,0:T(8,128)(2,1)S(1)}, bf16[288,128]{1,0:T(8,128)(2,1)S(1)}, u32[]{:S(2)}, u32[]{:S(2)}) collective-permute-start(bf16[288,128]{1,0:T(8,128)(2,1)S(1)} %get-tuple-element.136), channel_id=1, source_target_pairs={{0,6},{2,4},{4,2},{6,0},{8,14},{10,12},{12,10},{14,8},{1,7},{3,5},... | collective-permute-start | bytes 221192 | tf_op jit(solution)/shard_map/ppermute | solution.py:1046
